TPU v7x, 32 devices: a whole 2x2x4 slice. The times are simulated.
32 devices in a mesh: groups: 2 (over x), seq: 16 (over z, y, core).
Axes of the slice: x: 2, y: 2, z: 4, core: 2. Of those that a mesh axis runs over, the one named last changes fastest.
Arguments:
- queries: bfloat16 [16384, 4096], P(('groups', 'seq')), parts along dimension 0, may hold values from -80 to 80
- keys: bfloat16 [16384, 1024], P(('groups', 'seq')), parts along dimension 0, may hold values from -4 to 4
- values: bfloat16 [16384, 1024], P(('groups', 'seq')), parts along dimension 0, may hold values from -6 to 6
- doc_start: int32 [16384], P(('groups', 'seq')), parts along dimension 0, may hold values from 0 to 8191, as said below
- block_list: int32 [128, 8], P(('groups', 'seq')), parts along dimension 0, may hold values from -1 to 63, as said below
Outputs:
- attended: bfloat16 [16384, 4096], P(('groups', 'seq')), parts along dimension 0
There are 2 independent parts, one for each index of `groups`. A program takes and returns all parts, laid end to end along the dimension named above; each array names one. Nothing has to cross between parts.
Inputs may be any that keep to these rules, and one draw needn't show every extreme that they name: doc_start[i] <= i and i - doc_start[i] < 2048; doc_start never falls and changes only to i itself where a new document begins at i; some document holds exactly 2048 tokens; the window's last token begins a document of its own. `block_list`: row q names distinct key blocks, filled slots first and -1 after them; its first entry is q itself; every entry e satisfies q - 16 <= e <= q and lies at or after the block that holds doc_start of position q * 128; some row fills all 8 slots.
All inputs are finite; a program needn't handle non-finite values.
Results may differ from a plain program's by a relative error of at most 0.0045.
Values may be sent and summed in bfloat16 or wider, within the bound.
No kernel may reach another device: no remote copies, remote signals or barrier semaphores. Data moves between devices by JAX's collectives and lax.ppermute only.
A program may use at most 128 MiB of HBM per device.

v0:
```python
import jax
import jax.numpy as jnp
from jax import lax
from jax.sharding import PartitionSpec as P

HEAD_DIM = 128
SPAN = 4


NEG_BIG = -1e30


def from_behind(block, axis, distance):
    devices = range(lax.axis_size(axis))
    route = [(i - distance, i) for i in devices if i - distance in devices]
    return lax.ppermute(block, axis, route)


def build_window(stacked):
    pieces = [stacked]
    moving = stacked
    for distance in range(SPAN):
        moving = from_behind(moving, "seq", 1)
        pieces.append(moving)
    return jnp.stack(pieces[::-1], axis=1)


def block_scores(query_block, key_rows):
    return jnp.einsum(
        "qhgd,khd->hgqk", query_block, key_rows, preferred_element_type=jnp.float32
    ) * HEAD_DIM ** (-0.5)


def dense_block(query_block, starts, positions, entries, window_blocks, first_block, kv_count):
    block_rows = query_block.shape[0]
    filled = entries >= 0
    local_index = jnp.clip(entries - first_block, 0, window_blocks.shape[1] - 1)
    chosen = jnp.take(window_blocks, local_index, axis=1)
    key_rows = chosen[0].reshape(-1, kv_count, HEAD_DIM)
    value_rows = chosen[1].reshape(-1, kv_count, HEAD_DIM)
    key_pos = (
        entries[:, None] * block_rows + jnp.arange(block_rows, dtype=jnp.int32)[None, :]
    ).reshape(-1)
    key_live = jnp.repeat(filled, block_rows)
    allowed = (
        key_live[None, :]
        & (key_pos[None, :] >= starts[:, None])
        & (key_pos[None, :] <= positions[:, None])
    )
    scores = block_scores(query_block, key_rows)
    row_top = jnp.max(jnp.where(allowed, scores, NEG_BIG), axis=-1)
    weights = jnp.where(allowed, jnp.exp(scores - row_top[..., None]), 0.0)
    row_total = jnp.sum(weights, axis=-1)
    mixed_sum = jnp.einsum(
        "hgqk,khd->hgqd",
        weights.astype(jnp.bfloat16),
        value_rows,
        preferred_element_type=jnp.float32,
    )
    return mixed_sum / row_total[..., None]


def to_rows(result, block_rows):
    return jnp.transpose(result, (2, 0, 1, 3)).reshape(block_rows, -1).astype(jnp.bfloat16)


def local(queries, keys, values, doc_start, block_list):
    tokens_here = queries.shape[0]
    blocks_here = block_list.shape[0]
    block_rows = tokens_here // blocks_here
    kv_width = keys.shape[1]
    kv_count = kv_width // HEAD_DIM
    group_size = queries.shape[1] // kv_width
    stacked = jnp.stack([keys, values], axis=0)
    window = build_window(stacked)
    window_blocks = window.reshape(2, -1, block_rows, kv_width)
    my_index = lax.axis_index("seq")
    first_block = (my_index - SPAN) * blocks_here
    row_offsets = jnp.arange(block_rows, dtype=jnp.int32)

    def own_rows(block_id):
        query_block = lax.dynamic_slice_in_dim(queries, block_id * block_rows, block_rows, 0)
        query_block = query_block.reshape(block_rows, kv_count, group_size, HEAD_DIM)
        starts = lax.dynamic_slice_in_dim(doc_start, block_id * block_rows, block_rows, 0)
        positions = (my_index * blocks_here + block_id) * block_rows + row_offsets
        return (query_block, starts, positions, block_list[block_id])

    def dense_one(block_id):
        query_block, starts, positions, entries = own_rows(block_id)
        result = dense_block(
            query_block, starts, positions, entries, window_blocks, first_block, kv_count
        )
        return to_rows(result, block_rows)

    attended = lax.map(dense_one, jnp.arange(blocks_here, dtype=jnp.int32))
    return attended.reshape(tokens_here, -1)


def solution(mesh):
    return jax.shard_map(
        local,
        mesh=mesh,
        in_specs=(
            P(("groups", "seq"), None),
            P(("groups", "seq"), None),
            P(("groups", "seq"), None),
            P(("groups", "seq")),
            P(("groups", "seq"), None),
        ),
        out_specs=P(("groups", "seq"), None),
        check_vma=False,
    )
```

profile of v0, /device:TPU:24, one launch (start us, length us, event | category | flops | bytes accessed | tf_op | source)
XLA Modules:
  0.0 292.1 jit_solution(3424140498140903065)
XLA Ops:
  0.0 1.7 pad_maximum_fusion
  1.7 1.9 collective-permute-start
  3.7 26.3 %collective-permute-done = bf16[2,512,1024]{2,1,0:T(8,128)(2,1)S(1)} collective-permute-done((bf16[2,512,1024]{2,1,0:T(8,128)(2,1)S(1)}, bf16[2,512,1024]{2,1,0:T(8,128)(2,1)S(1)}, u32[]{:S(2)}, u32[]{:S(2)}) %collective-permute-start) | collective-permute-done | bytes 2097184 | tf_op jit(solution)/shard_map/ppermute | solution.py:16
  30.0 1.9 collective-permute-start.1
  31.9 26.3 %collective-permute-done.1 = bf16[2,512,1024]{2,1,0:T(8,128)(2,1)S(1)} collective-permute-done((bf16[2,512,1024]{2,1,0:T(8,128)(2,1)S(1)}, bf16[2,512,1024]{2,1,0:T(8,128)(2,1)S(1)}, u32[]{:S(2)}, u32[]{:S(2)}) %collective-permute-start.1) | collective-permute-done | bytes 2097184 | tf_op jit(solution)/shard_map/ppermute | solution.py:16
  58.2 1.4 copy-done.2
  59.6 1.9 collective-permute-start.2
  61.5 26.4 %collective-permute-done.2 = bf16[2,512,1024]{2,1,0:T(8,128)(2,1)} collective-permute-done((bf16[2,512,1024]{2,1,0:T(8,128)(2,1)S(1)}, bf16[2,512,1024]{2,1,0:T(8,128)(2,1)}, u32[]{:S(2)}, u32[]{:S(2)}) %collective-permute-start.2) | collective-permute-done | bytes 2097184 | tf_op jit(solution)/shard_map/ppermute | solution.py:16
  87.9 1.9 collective-permute-start.3
  89.9 26.6 %collective-permute-done.3 = bf16[2,512,1024]{2,1,0:T(8,128)(2,1)} collective-permute-done((bf16[2,512,1024]{2,1,0:T(8,128)(2,1)}, bf16[2,512,1024]{2,1,0:T(8,128)(2,1)}, u32[]{:S(2)}, u32[]{:S(2)}) %collective-permute-start.3) | collective-permute-done | bytes 2097184 | tf_op jit(solution)/shard_map/ppermute | solution.py:16
  116.5 3.1 %bitcast_dynamic-update-slice_fusion.4 = bf16[2,5,512,1024]{3,2,0,1:T(8,128)(2,1)} fusion(bf16[2,512,1024]{2,1,0:T(8,128)(2,1)} %collective-permute-done.3), kind=kLoop, calls=%fused_computation.44 | loop fusion | bytes 4194304
  119.6 3.1 %bitcast_dynamic-update-slice_fusion.3 = bf16[2,5,512,1024]{3,2,0,1:T(8,128)(2,1)} fusion(bf16[2,5,512,1024]{3,2,0,1:T(8,128)(2,1)} %bitcast_dynamic-update-slice_fusion.4, bf16[2,512,1024]{2,1,0:T(8,128)(2,1)} %collective-permute-done.2), kind=kLoop, calls=%fused_computation.43 | loop fusion | bytes 4194304
  122.7 1.5 bitcast_dynamic-update-slice_fusion.2
  124.2 1.5 bitcast_dynamic-update-slice_fusion.1
  125.7 1.5 bitcast_dynamic-update-slice_fusion
  127.2 9.2 %copy.14 = bf16[2,5,512,1024]{3,2,1,0:T(8,128)(2,1)} copy(bf16[2,5,512,1024]{3,2,0,1:T(8,128)(2,1)} %bitcast_dynamic-update-slice_fusion) | data formatting | bytes 20971520 | tf_op jit(solution)/shard_map/stack | solution.py:25
  136.4 155.8 %while.13 = (s32[]{:T(128)}, bf16[4,128,4096]{2,1,0:T(8,128)(2,1)}, s32[4]{0:T(128)S(1)}, s32[4,8]{1,0:T(4,128)}, s32[512]{0:T(512)}, /*index=5*/s32[]{:T(128)},...) while((s32[]{:T(128)}, bf16[4,128,4096]{2,1,0:T(8,128)(2,1)}, ...), condition=%wide.region_3.4_spmd.clone, body=%wide.region_0.3_spmd.clone.sunk | while | flops 3254258944 | bytes 65324656 | solution.py:95
  136.4 0.6 dynamic_slice.32
  137.5 0.8 dynamic_slice.33
  140.0 0.7 compare_and_fusion.4
  141.8 6.9 %gather_fusion = bf16[8,2,128,1024]{3,2,1,0:T(8,128)(2,1)} fusion(bf16[2,20,128,1024]{3,2,1,0:T(8,128)(2,1)} %get-tuple-element.279, s32[1024]{0:T(1024)S(1)} %pad_clamp_fusion.2), kind=kCustom, calls=%fused_computation.clone.clone.1 | custom fusion | bytes 8388640 | tf_op jit(solution)/shard_map/while/body/eval_jaxpr/jit(_take)/gather | solution.py:38
  148.7 2.7 select_bitcast_fusion.2
  151.8 1.9 copy.58
  153.7 1.3 constant_dynamic-slice_fusion.4
  155.0 1.3 copy.57
  156.3 12.0 %fusion.57 = (f32[8,4,128]{2,1,0:T(4,128)S(1)}, bf16[8,4,128,1024]{2,3,1,0:T(8,128)(2,1)}) fusion(pred[128,1024]{0,1:T(8,128)(4,1)S(1)} %compare_and_fusion.5, bf16[128,8,4,128]{0,3,2,1:T(8,128)(2,1)} %bitcast.116, bf16[1024,8,128,1]{2,1,0,3:T(8,128)(2,1)} %bitcast.114), kind=kOutput, calls=%fused_computation.46.clone.1 | convolution fusion | flops 2176844800 | bytes 11681792 | tf_op jit(solution)/shard_map/while/body/eval_jaxpr/sub | solution.py:52
  168.3 0.6 copy.59
  168.9 4.8 %fusion.58 = bf16[128,8,4,128]{0,3,2,1:T(8,128)(2,1)S(1)} fusion(bf16[8,4,128,1024]{2,3,1,0:T(8,128)(2,1)} %get-tuple-element.241, bf16[1024,8,128,1]{2,1,0,3:T(8,128)(2,1)S(1)} %bitcast.115, f32[128,8,4]{0,2,1:T(4,128)S(1)} %bitcast.122), kind=kOutput, calls=%fused_computation.17.clone.1 | convolution fusion | flops 1074790400 | bytes 11550720 | tf_op jit(solution)/shard_map/while/body/eval_jaxpr/hgqk,khd->hgqd/dot_general | solution.py:54
  174.3 1.0 constant_dynamic-update-slice_fusion.2
  175.3 0.6 dynamic_slice.32
  176.5 0.8 dynamic_slice.33
  178.9 0.7 compare_and_fusion.4
  180.7 6.9 %gather_fusion = bf16[8,2,128,1024]{3,2,1,0:T(8,128)(2,1)} fusion(bf16[2,20,128,1024]{3,2,1,0:T(8,128)(2,1)} %get-tuple-element.279, s32[1024]{0:T(1024)S(1)} %pad_clamp_fusion.2), kind=kCustom, calls=%fused_computation.clone.clone.1 | custom fusion | bytes 8388640 | tf_op jit(solution)/shard_map/while/body/eval_jaxpr/jit(_take)/gather | solution.py:38
  187.6 2.7 select_bitcast_fusion.2
  190.7 1.9 copy.58
  192.6 1.3 constant_dynamic-slice_fusion.4
  193.9 1.3 copy.57
  195.3 12.0 %fusion.57 = (f32[8,4,128]{2,1,0:T(4,128)S(1)}, bf16[8,4,128,1024]{2,3,1,0:T(8,128)(2,1)}) fusion(pred[128,1024]{0,1:T(8,128)(4,1)S(1)} %compare_and_fusion.5, bf16[128,8,4,128]{0,3,2,1:T(8,128)(2,1)} %bitcast.116, bf16[1024,8,128,1]{2,1,0,3:T(8,128)(2,1)} %bitcast.114), kind=kOutput, calls=%fused_computation.46.clone.1 | convolution fusion | flops 2176844800 | bytes 11681792 | tf_op jit(solution)/shard_map/while/body/eval_jaxpr/sub | solution.py:52
  207.3 0.6 copy.59
  207.9 4.8 %fusion.58 = bf16[128,8,4,128]{0,3,2,1:T(8,128)(2,1)S(1)} fusion(bf16[8,4,128,1024]{2,3,1,0:T(8,128)(2,1)} %get-tuple-element.241, bf16[1024,8,128,1]{2,1,0,3:T(8,128)(2,1)S(1)} %bitcast.115, f32[128,8,4]{0,2,1:T(4,128)S(1)} %bitcast.122), kind=kOutput, calls=%fused_computation.17.clone.1 | convolution fusion | flops 1074790400 | bytes 11550720 | tf_op jit(solution)/shard_map/while/body/eval_jaxpr/hgqk,khd->hgqd/dot_general | solution.py:54
  213.2 1.0 constant_dynamic-update-slice_fusion.2
  214.3 0.6 dynamic_slice.32
  215.4 0.8 dynamic_slice.33
  217.9 0.7 compare_and_fusion.4
  219.7 6.9 %gather_fusion = bf16[8,2,128,1024]{3,2,1,0:T(8,128)(2,1)} fusion(bf16[2,20,128,1024]{3,2,1,0:T(8,128)(2,1)} %get-tuple-element.279, s32[1024]{0:T(1024)S(1)} %pad_clamp_fusion.2), kind=kCustom, calls=%fused_computation.clone.clone.1 | custom fusion | bytes 8388640 | tf_op jit(solution)/shard_map/while/body/eval_jaxpr/jit(_take)/gather | solution.py:38
  226.5 2.7 select_bitcast_fusion.2
  229.6 1.9 copy.58
  231.6 1.3 constant_dynamic-slice_fusion.4
  232.9 1.3 copy.57
  234.2 12.0 %fusion.57 = (f32[8,4,128]{2,1,0:T(4,128)S(1)}, bf16[8,4,128,1024]{2,3,1,0:T(8,128)(2,1)}) fusion(pred[128,1024]{0,1:T(8,128)(4,1)S(1)} %compare_and_fusion.5, bf16[128,8,4,128]{0,3,2,1:T(8,128)(2,1)} %bitcast.116, bf16[1024,8,128,1]{2,1,0,3:T(8,128)(2,1)} %bitcast.114), kind=kOutput, calls=%fused_computation.46.clone.1 | convolution fusion | flops 2176844800 | bytes 11681792 | tf_op jit(solution)/shard_map/while/body/eval_jaxpr/sub | solution.py:52
  246.2 0.6 copy.59
  246.8 4.8 %fusion.58 = bf16[128,8,4,128]{0,3,2,1:T(8,128)(2,1)S(1)} fusion(bf16[8,4,128,1024]{2,3,1,0:T(8,128)(2,1)} %get-tuple-element.241, bf16[1024,8,128,1]{2,1,0,3:T(8,128)(2,1)S(1)} %bitcast.115, f32[128,8,4]{0,2,1:T(4,128)S(1)} %bitcast.122), kind=kOutput, calls=%fused_computation.17.clone.1 | convolution fusion | flops 1074790400 | bytes 11550720 | tf_op jit(solution)/shard_map/while/body/eval_jaxpr/hgqk,khd->hgqd/dot_general | solution.py:54
  252.2 1.0 constant_dynamic-update-slice_fusion.2
  254.4 0.8 dynamic_slice.33
  256.8 0.7 compare_and_fusion.4
  258.6 6.9 %gather_fusion = bf16[8,2,128,1024]{3,2,1,0:T(8,128)(2,1)} fusion(bf16[2,20,128,1024]{3,2,1,0:T(8,128)(2,1)} %get-tuple-element.279, s32[1024]{0:T(1024)S(1)} %pad_clamp_fusion.2), kind=kCustom, calls=%fused_computation.clone.clone.1 | custom fusion | bytes 8388640 | tf_op jit(solution)/shard_map/while/body/eval_jaxpr/jit(_take)/gather | solution.py:38
  265.5 2.7 select_bitcast_fusion.2
  268.6 1.9 copy.58
  270.5 1.3 constant_dynamic-slice_fusion.4
  271.8 1.3 copy.57
  273.1 12.0 %fusion.57 = (f32[8,4,128]{2,1,0:T(4,128)S(1)}, bf16[8,4,128,1024]{2,3,1,0:T(8,128)(2,1)}) fusion(pred[128,1024]{0,1:T(8,128)(4,1)S(1)} %compare_and_fusion.5, bf16[128,8,4,128]{0,3,2,1:T(8,128)(2,1)} %bitcast.116, bf16[1024,8,128,1]{2,1,0,3:T(8,128)(2,1)} %bitcast.114), kind=kOutput, calls=%fused_computation.46.clone.1 | convolution fusion | flops 2176844800 | bytes 11681792 | tf_op jit(solution)/shard_map/while/body/eval_jaxpr/sub | solution.py:52
  285.1 0.6 copy.59
  285.8 4.8 %fusion.58 = bf16[128,8,4,128]{0,3,2,1:T(8,128)(2,1)S(1)} fusion(bf16[8,4,128,1024]{2,3,1,0:T(8,128)(2,1)} %get-tuple-element.241, bf16[1024,8,128,1]{2,1,0,3:T(8,128)(2,1)S(1)} %bitcast.115, f32[128,8,4]{0,2,1:T(4,128)S(1)} %bitcast.122), kind=kOutput, calls=%fused_computation.17.clone.1 | convolution fusion | flops 1074790400 | bytes 11550720 | tf_op jit(solution)/shard_map/while/body/eval_jaxpr/hgqk,khd->hgqd/dot_general | solution.py:54
  291.1 1.0 constant_dynamic-update-slice_fusion.2
  (50 shorter events, 6.5 us)
Async XLA Ops:
  1.7 28.3 %collective-permute-start = (bf16[2,512,1024]{2,1,0:T(8,128)(2,1)S(1)}, bf16[2,512,1024]{2,1,0:T(8,128)(2,1)S(1)}, u32[]{:S(2)}, u32[]{:S(2)}) collective-permute-start(bf16[2,512,1024]{2,1,0:T(8,128)(2,1)S(1)} %pad_maximum_fusion), channel_id=1, source_target_pairs={{0,1},{1,2},{2,3},{3,4},{4,5},{5,6},{6,7},{7,8},{8,9},{9,10},{10,1... | collective-permute-start | bytes 6291464 | tf_op jit(solution)/shard_map/ppermute | solution.py:16
  30.0 28.2 %collective-permute-start.1 = (bf16[2,512,1024]{2,1,0:T(8,128)(2,1)S(1)}, bf16[2,512,1024]{2,1,0:T(8,128)(2,1)S(1)}, u32[]{:S(2)}, u32[]{:S(2)}) collective-permute-start(bf16[2,512,1024]{2,1,0:T(8,128)(2,1)S(1)} %collective-permute-done), channel_id=1, source_target_pairs={{0,1},{1,2},{2,3},{3,4},{4,5},{5,6},{6,7},{7,8},{8,9},{9,10},{10,1... | collective-permute-start | bytes 6291464 | tf_op jit(solution)/shard_map/ppermute | solution.py:16
  58.2 1.4 copy-start.2
  59.6 28.3 %collective-permute-start.2 = (bf16[2,512,1024]{2,1,0:T(8,128)(2,1)S(1)}, bf16[2,512,1024]{2,1,0:T(8,128)(2,1)}, u32[]{:S(2)}, u32[]{:S(2)}) collective-permute-start(bf16[2,512,1024]{2,1,0:T(8,128)(2,1)S(1)} %collective-permute-done.1), channel_id=1, source_target_pairs={{0,1},{1,2},{2,3},{3,4},{4,5},{5,6},{6,7},{7,8},{8,9},{9,10},{10,1... | collective-permute-start | bytes 6291464 | tf_op jit(solution)/shard_map/ppermute | solution.py:16
  87.9 28.6 %collective-permute-start.3 = (bf16[2,512,1024]{2,1,0:T(8,128)(2,1)}, bf16[2,512,1024]{2,1,0:T(8,128)(2,1)}, u32[]{:S(2)}, u32[]{:S(2)}) collective-permute-start(bf16[2,512,1024]{2,1,0:T(8,128)(2,1)} %collective-permute-done.2), channel_id=1, source_target_pairs={{0,1},{1,2},{2,3},{3,4},{4,5},{5,6},{6,7},{7,8},{8,9},{9,10},{10,1... | collective-permute-start | bytes 6291464 | tf_op jit(solution)/shard_map/ppermute | solution.py:16
  89.9 32.8 %copy-start.3 = (bf16[2,512,1024]{2,1,0:T(8,128)(2,1)S(1)}, bf16[2,512,1024]{2,1,0:T(8,128)(2,1)}, u32[]{:S(2)}) copy-start(bf16[2,512,1024]{2,1,0:T(8,128)(2,1)} %copy-done.2) | copy-start | bytes 6291460
  122.7 3.0 %copy-start = (bf16[512,1024]{1,0:T(8,128)(2,1)S(1)}, bf16[512,1024]{1,0:T(8,128)(2,1)}, u32[]{:S(2)}) copy-start(bf16[512,1024]{1,0:T(8,128)(2,1)} %param.9) | copy-start | bytes 3145732
  122.7 3.0 %copy-start.1 = (bf16[512,1024]{1,0:T(8,128)(2,1)S(1)}, bf16[512,1024]{1,0:T(8,128)(2,1)}, u32[]{:S(2)}) copy-start(bf16[512,1024]{1,0:T(8,128)(2,1)} %param.8) | copy-start | bytes 3145732
where the time goes:
time: 293 us; the launch traced here: 292 us
  waiting for transfers between devices  106 us (36%)
  local copies, waits for them, and re-layouts  81.6 us (28%)
  matrix products  67.2 us (23%)
  other arithmetic  18.4 us (6%)
  loops' own time  11.6 us (4%)
  starting transfers between devices  7.65 us (3%)
    ppermute x4, waiting for transfers between devices, from_behind(): return lax.ppermute(block, axis, route)  106 us
    sub x4, matrix products, dense_block(): weights = jnp.where(allowed, jnp.exp(scores - row_top[..., None]), 0.0)  48 us
    gather x4, local copies, waits for them, and re-layouts, dense_block(): chosen = jnp.take(window_blocks, local_index, axis=1)  27.4 us
    dot_general x4, matrix products, dense_block(): jnp.einsum('hgqk,khd->hgqd', weights.astype(jnp.bfloat16), value_rows, pr...  19.2 us
    another operation x1, loops' own time, local(): attended = lax.map(dense_one, jnp.arange(blocks_here, dtype=jnp.int32))  11.6 us
    select_n x8, other arithmetic, dense_block(): chosen = jnp.take(window_blocks, local_index, axis=1)  10.7 us
    unnamed x12, local copies, waits for them, and re-layouts  10.6 us
    dynamic_slice x8, local copies, waits for them, and re-layouts, own_rows(): lax.dynamic_slice_in_dim(queries, block_id * block_rows, block_rows, 0)  10.4 us
  transfers between devices with their start and end apart: 4, of which 4 were waited for; matrix products, arithmetic and copies ran while one was open for 0% of the time, Pallas kernels for 0%

commit v1 on v0

v1 whole, which is shorter than its diff:
```python
import functools

import jax
import jax.numpy as jnp
from jax import lax
from jax.experimental import pallas as pl
from jax.experimental.pallas import tpu as pltpu
from jax.sharding import PartitionSpec as P

HEAD_DIM = 128
BLOCK = 128
GROUP = 4
SHARDS = 5
PAIR = 2 * BLOCK
CHUNKS = (8,)
ROWS = 256
NEG_BIG = -1e30
LOG2E = 1.4426950408889634
SCALE = HEAD_DIM**-0.5 * LOG2E


def kernel(heads, aliased, table, bias, queries, *refs):
    sources = refs[:SHARDS]
    out, key_window, value_window, sems = refs[SHARDS + aliased :]
    step = pl.program_id(0)
    shard_rows = sources[0].shape[1]
    slots = bias.shape[1] // BLOCK
    blocks = bias.shape[0]

    def copies(head, slot):
        columns = pl.ds(pl.multiple_of(head * HEAD_DIM, HEAD_DIM), HEAD_DIM)
        made = []
        for n, source in enumerate(sources):
            rows = pl.ds(n * shard_rows, shard_rows)
            for m, window in enumerate((key_window, value_window)):
                made.append(
                    pltpu.make_async_copy(
                        source.at[m, :, columns], window.at[slot, rows, :], sems.at[slot, 2 * n + m]
                    )
                )
        return made

    slot = lax.rem(step, 2)

    @pl.when(step == 0)
    def _():
        for copy in copies(0, 0):
            copy.start()

    @pl.when(step + 1 < heads)
    def _():
        for copy in copies(step + 1, 1 - slot):
            copy.start()

    for copy in copies(step, slot):
        copy.wait()

    row_ids = lax.broadcasted_iota(jnp.int32, (BLOCK, BLOCK), 0)
    column_ids = lax.broadcasted_iota(jnp.int32, (BLOCK, BLOCK), 1)
    eye = (row_ids == column_ids).astype(jnp.bfloat16)
    per_pass = ROWS // BLOCK
    picker = jnp.concatenate([eye] * per_pass, 0)
    ones = jnp.ones((PAIR, HEAD_DIM), jnp.bfloat16)

    def block_rows(block_id, carry):
        first = pl.multiple_of(block_id * BLOCK, BLOCK)

        def pair_of(window, p):
            parts = []
            for j in (2 * p, 2 * p + 1):
                start = pl.multiple_of(table[block_id * slots + j] * BLOCK, BLOCK)
                parts.append(window[slot, pl.ds(start, BLOCK), :])
            return jnp.concatenate(parts, 0)

        for h0 in range(0, GROUP, per_pass):
            heads_now = range(h0, h0 + per_pass)
            rows = jnp.concatenate(
                [queries[pl.ds(first, BLOCK), h * HEAD_DIM : (h + 1) * HEAD_DIM] for h in heads_now], 0
            )
            rows = jnp.concatenate([rows, picker], 1)
            scores = []
            for p in range(slots // 2):
                masked_keys = jnp.concatenate(
                    [pair_of(key_window, p), bias[block_id, p * PAIR : (p + 1) * PAIR, :]], 1
                )
                scores.append(
                    lax.dot_general(
                        rows, masked_keys, (((1,), (1,)), ((), ())), preferred_element_type=jnp.float32
                    )
                )
            top = jnp.max(functools.reduce(jnp.maximum, scores), axis=1, keepdims=True)
            mixed = None
            for p in range(slots // 2):
                weights = jnp.exp2((scores[p] - top) * SCALE).astype(jnp.bfloat16)
                term = jnp.dot(
                    weights,
                    jnp.concatenate([pair_of(value_window, p), ones], 1),
                    preferred_element_type=jnp.float32,
                )
                mixed = term if mixed is None else mixed + term
            result = (mixed[:, :HEAD_DIM] / mixed[:, HEAD_DIM:]).astype(jnp.bfloat16)
            for n, h in enumerate(heads_now):
                out[pl.ds(first, BLOCK), h * HEAD_DIM : (h + 1) * HEAD_DIM] = result[
                    n * BLOCK : (n + 1) * BLOCK
                ]
        return carry

    lax.fori_loop(0, blocks, block_rows, 0)


def attend(table, bias, queries, sources, previous, first, heads):
    tokens, width = queries.shape
    group_width = GROUP * HEAD_DIM
    aliased = 0 if previous is None else 1
    anywhere = pl.BlockSpec(memory_space=pl.ANY)
    columns = pl.BlockSpec((tokens, group_width), lambda i, t: (0, first + i))
    work = tokens * GROUP * heads * bias.shape[1] * HEAD_DIM
    return pl.pallas_call(
        functools.partial(kernel, heads, aliased),
        grid_spec=pltpu.PrefetchScalarGridSpec(
            num_scalar_prefetch=1,
            grid=(heads,),
            in_specs=[pl.BlockSpec(bias.shape, lambda i, t: (0, 0, 0)), columns]
            + [anywhere] * (SHARDS + aliased),
            out_specs=columns,
            scratch_shapes=[
                pltpu.VMEM((2, SHARDS * tokens, HEAD_DIM), jnp.bfloat16),
                pltpu.VMEM((2, SHARDS * tokens, HEAD_DIM), jnp.bfloat16),
                pltpu.SemaphoreType.DMA((2, 2 * SHARDS)),
            ],
        ),
        out_shape=jax.ShapeDtypeStruct((tokens, width), jnp.bfloat16),
        input_output_aliases={3 + SHARDS: 0} if aliased else {},
        cost_estimate=pl.CostEstimate(
            flops=8 * work, bytes_accessed=4 * tokens * width, transcendentals=work // HEAD_DIM
        ),
        compiler_params=pltpu.CompilerParams(vmem_limit_bytes=32 << 20),
        name="attend",
    )(table, bias, queries, *sources, *(() if previous is None else (previous,)))


def masks(doc_start, block_list, shard):
    blocks = block_list.shape[0]
    offsets = jnp.arange(BLOCK, dtype=jnp.int32)
    starts = doc_start.reshape(blocks, 1, 1, BLOCK)
    places = ((shard * blocks + jnp.arange(blocks, dtype=jnp.int32))[:, None] * BLOCK + offsets)[
        :, None, None, :
    ]
    key_places = block_list[:, :, None, None] * BLOCK + offsets[:, None]
    allowed = (block_list >= 0)[:, :, None, None] & (key_places >= starts) & (key_places <= places)
    bias = jnp.where(allowed, 0.0, NEG_BIG).astype(jnp.bfloat16)
    return bias.reshape(blocks, -1, BLOCK)


def window_table(block_list, shard):
    blocks = block_list.shape[0]
    core = shard % 2
    entries = jnp.maximum(block_list, 0)
    behind = shard - entries // blocks
    nearest, third = jnp.where(core == 0, 4, 3), jnp.where(core == 0, 3, 4)
    place = jnp.where(behind == 1, nearest, 0)
    place = jnp.where(behind == 2, 1, place)
    place = jnp.where(behind == 3, third, place)
    place = jnp.where(behind == 4, 2, place)
    rows = place * blocks + entries % blocks
    return jnp.where(block_list >= 0, rows, 0).astype(jnp.int32).reshape(-1)


def local(queries, keys, values, doc_start, block_list):
    shard = lax.axis_index("seq")
    devices = range(lax.axis_size("seq"))
    core, row = shard % 2, (shard // 2) % 2
    two_back = [(i - 4, i) for i in devices if i >= 4]
    one_back = [(i ^ 2, i) for i in devices if i >= 2]
    sibling = [(i ^ 1, i) for i in devices]
    bias = masks(doc_start, block_list, shard)
    table = window_table(block_list, shard)
    out = None
    first = 0
    for heads in CHUNKS:
        columns = slice(first * HEAD_DIM, (first + heads) * HEAD_DIM)
        own = jnp.stack([keys[:, columns], values[:, columns]])
        from_z = lax.ppermute(own, "seq", two_back)
        from_y = lax.ppermute(jnp.where(row == 0, own, from_z), "seq", one_back)
        twin_x = lax.ppermute(jnp.where(core == 0, own, from_z), "seq", sibling)
        twin_y = lax.ppermute(from_y, "seq", sibling)
        out = attend(table, bias, queries, (own, from_y, from_z, twin_x, twin_y), out, first, heads)
        first += heads
    return out


def solution(mesh):
    shards = P(("groups", "seq"))
    return jax.shard_map(
        local,
        mesh=mesh,
        in_specs=(shards,) * 5,
        out_specs=shards,
        check_vma=False,
    )
```

time: 293 us -> 153 us (0.52)
  local copies, waits for them, and re-layouts: 81.6 us -> 2.45 us
  matrix products: 67.2 us -> 0 us
  Pallas kernels: 0 us -> 41.4 us
  loops' own time: 11.6 us -> 0 us
  other arithmetic: 18.4 us -> 7.51 us
  waiting for transfers between devices: 106 us -> 95.8 us
    sub x4 -> x0, matrix products: 48 us -> none  [dense_block(): weights = jnp.where(allowed, jnp.exp(scores - row_top[..., None]), 0.0)]
    pallas_call x0 -> x1, Pallas kernels: none -> 41.4 us  [attend(): pl.pallas_call(functools.partial(kernel, heads, aliased), grid_spec=pltpu...]
    gather x4 -> x0, local copies, waits for them, and re-layouts: 27.4 us -> none  [dense_block(): chosen = jnp.take(window_blocks, local_index, axis=1)]
    dot_general x4 -> x0, matrix products: 19.2 us -> none  [dense_block(): jnp.einsum('hgqk,khd->hgqd', weights.astype(jnp.bfloat16), value_rows, pr...]
    dynamic_slice x16 -> x0, local copies, waits for them, and re-layouts: 15.8 us -> none  [the longest x8 10.4 us: own_rows(): lax.dynamic_slice_in_dim(queries, block_id * block_rows, block_rows, 0)]
    another operation x1 -> x0, loops' own time: 11.6 us -> none  [local(): attended = lax.map(dense_one, jnp.arange(blocks_here, dtype=jnp.int32))]
    while x8 -> x0, local copies, waits for them, and re-layouts: 10.2 us -> none
    ppermute x4, waiting for transfers between devices: 106 us -> 95.8 us  [the longest x1 48.1 us: local(): from_z = lax.ppermute(own, 'seq', two_back)]
  transfers between devices with their start and end apart: 4 -> 4, of which waited for: 4 -> 3; matrix products, arithmetic and copies ran while one was open for 0% -> 1% of each run, Pallas kernels for 0% -> 0%
where the time goes in v1:
time: 153 us; the launch traced here: 152 us
  waiting for transfers between devices  95.8 us (63%)
  Pallas kernels  41.4 us (27%)
  other arithmetic  7.51 us (5%)
  starting transfers between devices  4.77 us (3%)
  local copies, waits for them, and re-layouts  2.45 us (2%)
    ppermute x1, waiting for transfers between devices, local(): from_z = lax.ppermute(own, 'seq', two_back)  48.1 us
    ppermute x1, waiting for transfers between devices, local(): from_y = lax.ppermute(jnp.where(row == 0, own, from_z), 'seq', one_back)  45 us
    pallas_call x1, Pallas kernels, attend(): pl.pallas_call(functools.partial(kernel, heads, aliased), grid_spec=pltpu...  41.4 us
    ppermute x1, starting transfers between devices, local(): from_y = lax.ppermute(jnp.where(row == 0, own, from_z), 'seq', one_back)  3.42 us
    another operation x1, other arithmetic, local(): own = jnp.stack([keys[:, columns], values[:, columns]])  3.16 us
  transfers between devices with their start and end apart: 4, of which 3 were waited for; matrix products, arithmetic and copies ran while one was open for 1% of the time, Pallas kernels for 0%

profile of v1, /device:TPU:24, one launch (start us, length us, event | category | flops | bytes accessed | tf_op | source)
XLA Modules:
  0.0 152.0 jit_solution(9838681671670762737)
XLA Ops:
  0.0 0.0 copy-start.1
  0.0 3.2 %pad_maximum_fusion.refs_0_ = bf16[2,512,1024]{2,1,0:T(8,128)(2,1)} fusion(bf16[1,512,1024]{2,1,0:T(8,128)(2,1)} %bitcast.14, bf16[1,512,1024]{2,1,0:T(8,128)(2,1)} %bitcast.16), kind=kLoop, calls=%fused_computation | loop fusion | flops 1048576 | bytes 4194304 | tf_op jit(solution)/shard_map/stack | solution.py:182
  3.2 1.3 collective-permute-start
  4.5 0.0 copy-start.2
  4.5 0.0 copy-start.3
  4.5 48.1 %collective-permute-done.refs_2_ = bf16[2,512,1024]{2,1,0:T(8,128)(2,1)S(1)} collective-permute-done((bf16[2,512,1024]{2,1,0:T(8,128)(2,1)}, bf16[2,512,1024]{2,1,0:T(8,128)(2,1)S(1)}, u32[]{:S(2)}, u32[]{:S(2)}) %collective-permute-start) | collective-permute-done | bytes 2097184 | tf_op jit(solution)/shard_map/ppermute | solution.py:183
  52.6 0.0 copy-done.1
  52.6 2.8 %broadcast_select_fusion = (bf16[2,512,1024]{2,1,0:T(8,128)(2,1)}, bf16[2,512,1024]{2,1,0:T(8,128)(2,1)S(1)}) fusion(bf16[2,512,1024]{2,1,0:T(8,128)(2,1)S(1)} %collective-permute-done.refs_2_, pred[]{:T(512)S(6)} %eq.31, bf16[1,512,1024]{2,1,0:T(8,128)(2,1)S(1)} %bitcast.15, bf16[1,512,1024]{2,1,0:T(8,128)(2,1)} %bitcast.17, pred[]{:T(512)S(6)} %eq.34), kind=kLoop, calls=%fused_computation.2 | loop fusion | flops 3145728 | bytes 8388610 | tf_op jit(solution)/shard_map/jit(_where)/select_n | solution.py:185
  55.4 3.4 %collective-permute-start.1 = (bf16[2,512,1024]{2,1,0:T(8,128)(2,1)S(1)}, bf16[2,512,1024]{2,1,0:T(8,128)(2,1)}, u32[]{:S(2)}, u32[]{:S(2)}) collective-permute-start(bf16[2,512,1024]{2,1,0:T(8,128)(2,1)S(1)} %get-tuple-element.6), channel_id=1, source_target_pairs={{0,2},{1,3},{6,4},{7,5},{4,6},{5,7},{10,8},{11,9},{8,10},{9,11},{1... | collective-permute-start | bytes 6291464 | tf_op jit(solution)/shard_map/ppermute | solution.py:184
  58.9 0.1 collective-permute-start.2
  59.0 45.0 %collective-permute-done.1.refs_1_ = bf16[2,512,1024]{2,1,0:T(8,128)(2,1)} collective-permute-done((bf16[2,512,1024]{2,1,0:T(8,128)(2,1)S(1)}, bf16[2,512,1024]{2,1,0:T(8,128)(2,1)}, u32[]{:S(2)}, u32[]{:S(2)}) %collective-permute-start.1) | collective-permute-done | bytes 2097184 | tf_op jit(solution)/shard_map/ppermute | solution.py:184
  103.9 0.0 collective-permute-start.3
  104.0 0.0 copy-done.2
  104.0 0.1 reshape.45.table
  104.1 0.1 broadcast_bitcast_fusion.1
  104.2 0.1 iota_add_fusion
  104.2 0.1 broadcast_bitcast_fusion
  104.3 0.0 copy-done.3
  104.3 1.4 select_convert_fusion.bias
  105.8 0.0 collective-permute-done.2.refs_3_
  105.8 2.7 %collective-permute-done.3.refs_4_ = bf16[2,512,1024]{2,1,0:T(8,128)(2,1)} collective-permute-done((bf16[2,512,1024]{2,1,0:T(8,128)(2,1)}, bf16[2,512,1024]{2,1,0:T(8,128)(2,1)}, u32[]{:S(2)}, u32[]{:S(2)}) %collective-permute-start.3) | collective-permute-done | bytes 2097184 | tf_op jit(solution)/shard_map/ppermute | solution.py:186
  108.5 0.0 copy-start
  108.5 2.2 %copy-done = bf16[512,4096]{1,0:T(8,128)(2,1)S(1)} copy-done((bf16[512,4096]{1,0:T(8,128)(2,1)S(1)}, bf16[512,4096]{1,0:T(8,128)(2,1)}, u32[]{:S(2)}) %copy-start) | copy-done | bytes 4194328
  110.6 41.4 %attend.1 = bf16[512,4096]{1,0:T(8,128)(2,1)} custom-call(s32[32]{0:T(128)S(1)} %reshape.45.table, bf16[4,1024,128]{2,1,0:T(8,128)(2,1)S(1)} %select_convert_fusion.bias, bf16[512,4096]{1,0:T(8,128)(2,1)S(1)} %copy-done, bf16[2,512,1024]{2,1,0:T(8,128)(2,1)} %pad_maximum_fusion.refs_0_, bf16[2,512,1024]{2,1,0:T(8,128)(2,1)} %collective-permute-done.1.refs_1_, ...), custom_call_target="tpu_custom_call" | custom-call | flops 17179869184 | bytes 8388608 | tf_op jit(solution)/shard_map/attend/pallas_call | solution.py:118
  (6 shorter events, 0.1 us)
Async XLA Ops:
  0.0 52.6 %copy-start.1 = (bf16[512,1024]{1,0:T(8,128)(2,1)S(1)}, bf16[512,1024]{1,0:T(8,128)(2,1)}, u32[]{:S(2)}) copy-start(bf16[512,1024]{1,0:T(8,128)(2,1)} %param.7) | copy-start | bytes 3145732
  3.2 49.5 %collective-permute-start = (bf16[2,512,1024]{2,1,0:T(8,128)(2,1)}, bf16[2,512,1024]{2,1,0:T(8,128)(2,1)S(1)}, u32[]{:S(2)}, u32[]{:S(2)}) collective-permute-start(bf16[2,512,1024]{2,1,0:T(8,128)(2,1)} %pad_maximum_fusion.refs_0_), channel_id=1, source_target_pairs={{0,4},{1,5},{2,6},{3,7},{4,8},{5,9},{6,10},{7,11},{8,12},{9,13},{1... | collective-permute-start | bytes 6291464 | tf_op jit(solution)/shard_map/ppermute | solution.py:183
  4.5 99.5 %copy-start.2 = (s32[4,8]{1,0:T(4,128)S(1)}, s32[4,8]{1,0:T(4,128)}, u32[]{:S(2)}) copy-start(s32[4,8]{1,0:T(4,128)} %param.9) | copy-start | bytes 388
  4.5 99.8 %copy-start.3 = (s32[512]{0:T(512)S(1)}, s32[512]{0:T(512)}, u32[]{:S(2)}) copy-start(s32[512]{0:T(512)} %param.8) | copy-start | bytes 6148
  55.4 48.5 %collective-permute-start.1 = (bf16[2,512,1024]{2,1,0:T(8,128)(2,1)S(1)}, bf16[2,512,1024]{2,1,0:T(8,128)(2,1)}, u32[]{:S(2)}, u32[]{:S(2)}) collective-permute-start(bf16[2,512,1024]{2,1,0:T(8,128)(2,1)S(1)} %get-tuple-element.6), channel_id=1, source_target_pairs={{0,2},{1,3},{6,4},{7,5},{4,6},{5,7},{10,8},{11,9},{8,10},{9,11},{1... | collective-permute-start | bytes 6291464 | tf_op jit(solution)/shard_map/ppermute | solution.py:184
  58.9 46.9 %collective-permute-start.2 = (bf16[2,512,1024]{2,1,0:T(8,128)(2,1)}, bf16[2,512,1024]{2,1,0:T(8,128)(2,1)}, u32[]{:S(2)}, u32[]{:S(2)}) collective-permute-start(bf16[2,512,1024]{2,1,0:T(8,128)(2,1)} %get-tuple-element.5), channel_id=1, source_target_pairs={{1,0},{0,1},{3,2},{2,3},{5,4},{4,5},{7,6},{6,7},{9,8},{8,9},{11,10... | collective-permute-start | bytes 6291464 | tf_op jit(solution)/shard_map/ppermute | solution.py:185
  103.9 4.5 %collective-permute-start.3 = (bf16[2,512,1024]{2,1,0:T(8,128)(2,1)}, bf16[2,512,1024]{2,1,0:T(8,128)(2,1)}, u32[]{:S(2)}, u32[]{:S(2)}) collective-permute-start(bf16[2,512,1024]{2,1,0:T(8,128)(2,1)} %collective-permute-done.1.refs_1_), channel_id=1, source_target_pairs={{1,0},{0,1},{3,2},{2,3},{5,4},{4,5},{7,6},{6,7},{9,8},{8,9},{11,10... | collective-permute-start | bytes 6291464 | tf_op jit(solution)/shard_map/ppermute | solution.py:186
  108.5 2.2 %copy-start = (bf16[512,4096]{1,0:T(8,128)(2,1)S(1)}, bf16[512,4096]{1,0:T(8,128)(2,1)}, u32[]{:S(2)}) copy-start(bf16[512,4096]{1,0:T(8,128)(2,1)} %queries.1) | copy-start | bytes 12582916

commit v2 on v1

v2 whole, which is shorter than its diff:
```python
import functools

import jax
import jax.numpy as jnp
from jax import lax
from jax.experimental import pallas as pl
from jax.experimental.pallas import tpu as pltpu
from jax.sharding import PartitionSpec as P


HEAD_DIM = 128
BLOCK = 128
GROUP = 4
SHARDS = 5
PAIR = 2 * BLOCK
CHUNKS = (1, 2, 2, 2, 1)
SUBLANES = 16
VMEM_LIMIT = 32 << 20
NEG_BIG = -1e30
LOG2E = 1.4426950408889634
SCALE = HEAD_DIM**-0.5 * LOG2E


def kernel(aliased, table, bias, queries, *refs):
    sources = refs[:SHARDS]
    out, key_window, value_window, scores, weights, tops = refs[SHARDS + aliased :]
    step = pl.program_id(0)
    blocks, listed = bias.shape[0], bias.shape[1]
    slots = listed // BLOCK
    shard_rows = sources[0].shape[2]
    width = GROUP * HEAD_DIM
    for m, window in enumerate((key_window, value_window)):
        for n, source in enumerate(sources):
            window[n * shard_rows : (n + 1) * shard_rows, :] = source[step, m]

    row_ids = lax.broadcasted_iota(jnp.int32, (BLOCK, BLOCK), 0)
    column_ids = lax.broadcasted_iota(jnp.int32, (BLOCK, BLOCK), 1)
    eye = (row_ids == column_ids).astype(jnp.bfloat16)
    picker = jnp.concatenate([eye] * GROUP, 0)
    ones = jnp.ones((SUBLANES, listed), jnp.bfloat16)

    def parts(window, block_id):
        made = []
        for j in range(slots):
            start = pl.multiple_of(table[block_id * slots + j] * BLOCK, BLOCK)
            made.append(window[pl.ds(start, BLOCK), :])
        return made

    def score(block_id, b):
        rows = slice(block_id * BLOCK, (block_id + 1) * BLOCK)
        stacked = [queries[rows, h * HEAD_DIM : (h + 1) * HEAD_DIM] for h in range(GROUP)]
        found = lax.dot_general(
            jnp.concatenate([jnp.concatenate(parts(key_window, block_id), 0), bias[block_id]], 1),
            jnp.concatenate([jnp.concatenate(stacked, 0), picker], 1),
            (((1,), (1,)), ((), ())),
            preferred_element_type=jnp.float32,
        )
        scores[b] = found
        tops[b] = jnp.max(found.reshape(-1, 8, width), axis=0)

    def soften(b):
        top = jnp.max(tops[b], axis=0, keepdims=True)
        for p in range(0, listed, PAIR):
            rows = slice(p, p + PAIR)
            weights[b, rows] = jnp.exp2((scores[b, rows] - top) * SCALE).astype(jnp.bfloat16)

    def mix(block_id, b):
        mixed = jnp.dot(
            jnp.concatenate([jnp.concatenate(parts(value_window, block_id), 1), ones], 0),
            weights[b],
            preferred_element_type=jnp.float32,
        )
        result = mixed[:HEAD_DIM] * (1.0 / mixed[HEAD_DIM : HEAD_DIM + 1])
        rows = slice(block_id * BLOCK, (block_id + 1) * BLOCK)
        for h in range(GROUP):
            columns = slice(h * HEAD_DIM, (h + 1) * HEAD_DIM)
            out[rows, columns] = result[:, h * BLOCK : (h + 1) * BLOCK].T.astype(jnp.bfloat16)

    for t in range(blocks + 2):
        if t < blocks:
            score(t, t % 2)
        if 0 <= t - 1 < blocks:
            soften((t - 1) % 2)
        if 0 <= t - 2 < blocks:
            mix(t - 2, (t - 2) % 2)


def attend(table, bias, queries, sources, previous, first, heads):
    tokens, width = queries.shape
    listed = bias.shape[1]
    group_width = GROUP * HEAD_DIM
    aliased = 0 if previous is None else 1
    near = pl.BlockSpec(memory_space=pltpu.VMEM)
    columns = pl.BlockSpec((tokens, group_width), lambda i, t: (0, first + i))
    work = tokens * GROUP * heads * listed * HEAD_DIM
    return pl.pallas_call(
        functools.partial(kernel, aliased),
        grid_spec=pltpu.PrefetchScalarGridSpec(
            num_scalar_prefetch=1,
            grid=(heads,),
            in_specs=[near, columns] + [near] * SHARDS + [pl.BlockSpec(memory_space=pl.ANY)] * aliased,
            out_specs=columns,
            scratch_shapes=[
                pltpu.VMEM((SHARDS * tokens, HEAD_DIM), jnp.bfloat16),
                pltpu.VMEM((SHARDS * tokens, HEAD_DIM), jnp.bfloat16),
                pltpu.VMEM((2, listed, group_width), jnp.float32),
                pltpu.VMEM((2, listed, group_width), jnp.bfloat16),
                pltpu.VMEM((2, 8, group_width), jnp.float32),
            ],
        ),
        out_shape=jax.ShapeDtypeStruct((tokens, width), jnp.bfloat16),
        input_output_aliases={3 + SHARDS: 0} if aliased else {},
        cost_estimate=pl.CostEstimate(
            flops=8 * work, bytes_accessed=4 * tokens * width, transcendentals=work // HEAD_DIM
        ),
        compiler_params=pltpu.CompilerParams(vmem_limit_bytes=VMEM_LIMIT),
        name="attend",
    )(table, bias, pltpu.with_memory_space_constraint(queries, pltpu.HBM), *sources, *(() if previous is None else (previous,)))


def plan_kernel(place, listed, starts, bias, table):
    shard = place[0]
    blocks, slots = listed.shape
    core = shard % 2
    shape = (BLOCK, BLOCK)
    key_offsets = lax.broadcasted_iota(jnp.int32, shape, 0)
    row_offsets = lax.broadcasted_iota(jnp.int32, shape, 1)
    for b in range(blocks):
        places = (shard * blocks + b) * BLOCK + row_offsets
        begins = jnp.broadcast_to(starts[b : b + 1, :], shape)
        for j in range(slots):
            entry = listed[b, j]
            key_places = entry * BLOCK + key_offsets
            allowed = (key_places >= begins) & (key_places <= places) & (entry >= 0)
            bias[b, j * BLOCK : (j + 1) * BLOCK, :] = jnp.where(allowed, 0.0, NEG_BIG).astype(jnp.bfloat16)
            known = jnp.maximum(entry, 0)
            shard_of = lax.div(known, blocks)
            behind = shard - shard_of
            where = jnp.where(behind == 1, 4 - core, 0)
            where = jnp.where(behind == 2, 1, where)
            where = jnp.where(behind == 3, 3 + core, where)
            where = jnp.where(behind == 4, 2, where)
            where = jnp.where(entry >= 0, where, 0)
            table[b * slots + j] = where * blocks + known - shard_of * blocks


def plan(doc_start, block_list, shard):
    blocks, slots = block_list.shape
    scalars, vectors = pl.BlockSpec(memory_space=pltpu.SMEM), pl.BlockSpec(memory_space=pltpu.VMEM)
    return pl.pallas_call(
        plan_kernel,
        in_specs=[scalars, scalars, vectors],
        out_specs=[vectors, scalars],
        out_shape=[
            jax.ShapeDtypeStruct((blocks, slots * BLOCK, BLOCK), jnp.bfloat16),
            jax.ShapeDtypeStruct((blocks * slots,), jnp.int32),
        ],
        compiler_params=pltpu.CompilerParams(vmem_limit_bytes=VMEM_LIMIT),
        name="plan",
    )(shard.reshape(1), block_list, doc_start.reshape(blocks, BLOCK))


def pack_kernel(spans, keys, values, *outs):
    for (first, heads), out in zip(spans, outs):
        for h in range(heads):
            columns = slice((first + h) * HEAD_DIM, (first + h + 1) * HEAD_DIM)
            out[h, 0] = keys[:, columns]
            for b in range(0, keys.shape[0], BLOCK):
                out[h, 1, b : b + BLOCK, :] = values[b : b + BLOCK, columns].T


def pack(keys, values, spans):
    tokens = keys.shape[0]
    width = sum(heads for _, heads in spans) * HEAD_DIM
    taken = pl.BlockSpec((tokens, width if spans[0][0] == 0 else keys.shape[1]), lambda i: (0, 0))
    shapes = [(heads, 2, tokens, HEAD_DIM) for _, heads in spans]
    return pl.pallas_call(
        functools.partial(pack_kernel, spans),
        grid=(1,),
        in_specs=[taken, taken],
        out_specs=[pl.BlockSpec(shape, lambda i: (0, 0, 0, 0)) for shape in shapes],
        out_shape=[jax.ShapeDtypeStruct(shape, keys.dtype) for shape in shapes],
        compiler_params=pltpu.CompilerParams(vmem_limit_bytes=VMEM_LIMIT),
        name="pack",
    )(*(pltpu.with_memory_space_constraint(x, pltpu.HBM) for x in (keys, values)))


def routed(queries, keys, values, doc_start, block_list):
    shard = lax.axis_index("seq")
    devices = range(lax.axis_size("seq"))
    core, row = shard % 2, (shard // 2) % 2
    two_back = [(i - 4, i) for i in devices if i >= 4]
    one_back = [(i ^ 2, i) for i in devices if i >= 2]
    sibling = [(i ^ 1, i) for i in devices]
    bias, table = plan(doc_start, block_list, shard)
    firsts = [sum(CHUNKS[:n]) for n in range(len(CHUNKS))]
    spans = list(zip(firsts, CHUNKS))
    owns = pack(keys, values, spans[:1]) + pack(keys, values, spans[1:])
    from_z = []
    for n in range(len(CHUNKS)):
        from_z.append(lax.ppermute(owns[n], "seq", two_back))
    out = None
    for n, heads in enumerate(CHUNKS):
        own, back = owns[n], from_z[n]
        from_y = lax.ppermute(jnp.where(row == 0, own, back), "seq", one_back)
        twin_x = lax.ppermute(jnp.where(core == 0, own, back), "seq", sibling)
        twin_y = lax.ppermute(from_y, "seq", sibling)
        out = attend(table, bias, queries, (own, from_y, back, twin_x, twin_y), out, firsts[n], heads)
    return out


def solution(mesh):
    shards = P(("groups", "seq"))
    return jax.shard_map(
        routed,
        mesh=mesh,
        in_specs=(shards,) * 5,
        out_specs=shards,
        check_vma=False,
    )
```

time: 153 us -> 107 us (0.70)
  waiting for transfers between devices: 95.8 us -> 35.3 us
  starting transfers between devices: 4.77 us -> 25.8 us
  other arithmetic: 7.51 us -> 2.28 us
  local copies, waits for them, and re-layouts: 2.45 us -> 0.01 us
    ppermute x4 -> x20, waiting for transfers between devices: 95.8 us -> 35.3 us  [the longest x5 30.1 us: routed(): from_z.append(lax.ppermute(owns[n], 'seq', two_back))]
    ppermute x4 -> x20, starting transfers between devices: 4.77 us -> 25.8 us  [the longest x5 17.3 us: routed(): from_y = lax.ppermute(jnp.where(row == 0, own, back), 'seq', one_back)]
    another operation x1 -> x0, other arithmetic: 3.16 us -> none  [local(): own = jnp.stack([keys[:, columns], values[:, columns]])]
    unnamed x11 -> x4, local copies, waits for them, and re-layouts: 2.36 us -> 0.01 us
    pallas_call x1 -> x8, Pallas kernels: 41.4 us -> 42.1 us  [the longest x5 36.9 us: attend(): pl.pallas_call(functools.partial(kernel, aliased), grid_spec=pltpu.Prefet...]
  transfers between devices with their start and end apart: 4 -> 20, of which waited for: 3 -> 5; matrix products, arithmetic and copies ran while one was open for 1% -> 2% of each run, Pallas kernels for 0% -> 32%
where the time goes in v2:
time: 107 us; the launch traced here: 106 us
  Pallas kernels  42.1 us (39%)
  waiting for transfers between devices  35.3 us (33%)
  starting transfers between devices  25.8 us (24%)
  other arithmetic  2.28 us (2%)
    pallas_call x5, Pallas kernels, attend(): pl.pallas_call(functools.partial(kernel, aliased), grid_spec=pltpu.Prefet...  36.9 us
    ppermute x5, waiting for transfers between devices, routed(): from_z.append(lax.ppermute(owns[n], 'seq', two_back))  30.1 us
    ppermute x5, starting transfers between devices, routed(): from_y = lax.ppermute(jnp.where(row == 0, own, back), 'seq', one_back)  17.3 us
    ppermute x5, starting transfers between devices, routed(): from_z.append(lax.ppermute(owns[n], 'seq', two_back))  6.45 us
    ppermute x5, waiting for transfers between devices, routed(): from_y = lax.ppermute(jnp.where(row == 0, own, back), 'seq', one_back)  5.16 us
    pallas_call x2, Pallas kernels, pack(): pl.pallas_call(functools.partial(pack_kernel, spans), grid=(1,), in_specs...  3.74 us
    select_n x5, other arithmetic, routed(): twin_x = lax.ppermute(jnp.where(core == 0, own, back), 'seq', sibling)  2.28 us
  transfers between devices with their start and end apart: 20, of which 5 were waited for; matrix products, arithmetic and copies ran while one was open for 2% of the time, Pallas kernels for 32%

profile of v2, /device:TPU:24, one launch (start us, length us, event | category | flops | bytes accessed | tf_op | source)
XLA Modules:
  0.0 105.7 jit_solution(8257694492859958716)
XLA Ops:
  0.0 2.7 %pack.2 = (bf16[2,2,512,128]{3,2,1,0:T(8,128)(2,1)S(1)}, bf16[2,2,512,128]{3,2,1,0:T(8,128)(2,1)S(1)}, bf16[2,2,512,128]{3,2,1,0:T(8,128)(2,1)S(1)}, bf16[1,2,512,128]{3,2,1,0:T(8,128)(2,1)}) custom-call(bf16[512,1024]{1,0:T(8,128)(2,1)} %keys.3, bf16[512,1024]{1,0:T(8,128)(2,1)} %values.3), custom_call_target="tpu_custom_call" | custom-call | tf_op jit(solution)/shard_map/pack/pallas_call | solution.py:177
  2.7 1.3 %collective-permute-start.12 = (bf16[2,2,512,128]{3,2,1,0:T(8,128)(2,1)S(1)}, bf16[2,2,512,128]{3,2,1,0:T(8,128)(2,1)S(1)}, u32[]{:S(2)}, u32[]{:S(2)}) collective-permute-start(bf16[2,2,512,128]{3,2,1,0:T(8,128)(2,1)S(1)} %get-tuple-element.16.refs_0_), channel_id=1, source_target_pairs={{0,4},{1,5},{2,6},{3,7},{4,8},{5,9},{6,10},{7,11},{8,12},{9,13},{1... | collective-permute-start | bytes 1572872 | tf_op jit(solution)/shard_map/ppermute | solution.py:201
  4.0 1.1 %pack.3.refs_0_ = bf16[1,2,512,128]{3,2,1,0:T(8,128)(2,1)S(1)} custom-call(bf16[512,1024]{1,0:T(8,128)(2,1)} %keys.3, bf16[512,1024]{1,0:T(8,128)(2,1)} %values.3), custom_call_target="tpu_custom_call" | custom-call | tf_op jit(solution)/shard_map/pack/pallas_call | solution.py:177
  5.0 0.0 copy-start
  5.1 0.0 copy-start.1
  5.1 1.3 %collective-permute-start.16 = (bf16[1,2,512,128]{3,2,1,0:T(8,128)(2,1)S(1)}, bf16[1,2,512,128]{3,2,1,0:T(8,128)(2,1)}, u32[]{:S(2)}, u32[]{:S(2)}) collective-permute-start(bf16[1,2,512,128]{3,2,1,0:T(8,128)(2,1)S(1)} %pack.3.refs_0_), channel_id=1, source_target_pairs={{0,4},{1,5},{2,6},{3,7},{4,8},{5,9},{6,10},{7,11},{8,12},{9,13},{1... | collective-permute-start | bytes 786440 | tf_op jit(solution)/shard_map/ppermute | solution.py:201
  6.4 1.3 %collective-permute-start.8 = (bf16[2,2,512,128]{3,2,1,0:T(8,128)(2,1)S(1)}, bf16[2,2,512,128]{3,2,1,0:T(8,128)(2,1)S(1)}, u32[]{:S(2)}, u32[]{:S(2)}) collective-permute-start(bf16[2,2,512,128]{3,2,1,0:T(8,128)(2,1)S(1)} %get-tuple-element.15.refs_0_), channel_id=1, source_target_pairs={{0,4},{1,5},{2,6},{3,7},{4,8},{5,9},{6,10},{7,11},{8,12},{9,13},{1... | collective-permute-start | bytes 1572872 | tf_op jit(solution)/shard_map/ppermute | solution.py:201
  7.7 1.3 %collective-permute-start.4 = (bf16[2,2,512,128]{3,2,1,0:T(8,128)(2,1)S(1)}, bf16[2,2,512,128]{3,2,1,0:T(8,128)(2,1)S(1)}, u32[]{:S(2)}, u32[]{:S(2)}) collective-permute-start(bf16[2,2,512,128]{3,2,1,0:T(8,128)(2,1)S(1)} %get-tuple-element.14.refs_0_), channel_id=1, source_target_pairs={{0,4},{1,5},{2,6},{3,7},{4,8},{5,9},{6,10},{7,11},{8,12},{9,13},{1... | collective-permute-start | bytes 1572872 | tf_op jit(solution)/shard_map/ppermute | solution.py:201
  9.0 1.3 %collective-permute-start = (bf16[1,2,512,128]{3,2,1,0:T(8,128)(2,1)}, bf16[1,2,512,128]{3,2,1,0:T(8,128)(2,1)}, u32[]{:S(2)}, u32[]{:S(2)}) collective-permute-start(bf16[1,2,512,128]{3,2,1,0:T(8,128)(2,1)} %get-tuple-element.13.refs_0_), channel_id=1, source_target_pairs={{0,4},{1,5},{2,6},{3,7},{4,8},{5,9},{6,10},{7,11},{8,12},{9,13},{1... | collective-permute-start | bytes 786440 | tf_op jit(solution)/shard_map/ppermute | solution.py:201
  10.3 14.8 %collective-permute-done.16.refs_2_ = bf16[1,2,512,128]{3,2,1,0:T(8,128)(2,1)} collective-permute-done((bf16[1,2,512,128]{3,2,1,0:T(8,128)(2,1)S(1)}, bf16[1,2,512,128]{3,2,1,0:T(8,128)(2,1)}, u32[]{:S(2)}, u32[]{:S(2)}) %collective-permute-start.16) | collective-permute-done | bytes 262176 | tf_op jit(solution)/shard_map/ppermute | solution.py:201
  25.1 1.0 broadcast_select_fusion.6
  26.1 3.4 %collective-permute-start.17 = (bf16[1,2,512,128]{3,2,1,0:T(8,128)(2,1)S(1)}, bf16[1,2,512,128]{3,2,1,0:T(8,128)(2,1)S(1)}, u32[]{:S(2)}, u32[]{:S(2)}) collective-permute-start(bf16[1,2,512,128]{3,2,1,0:T(8,128)(2,1)S(1)} %get-tuple-element.24), channel_id=1, source_target_pairs={{0,2},{1,3},{6,4},{7,5},{4,6},{5,7},{10,8},{11,9},{8,10},{9,11},{1... | collective-permute-start | bytes 786440 | tf_op jit(solution)/shard_map/ppermute | solution.py:205
  29.5 0.0 collective-permute-done.12.refs_2_
  29.5 0.1 collective-permute-start.18
  29.6 0.1 broadcast_select_fusion
  29.7 6.5 %collective-permute-done.8.refs_2_ = bf16[2,2,512,128]{3,2,1,0:T(8,128)(2,1)S(1)} collective-permute-done((bf16[2,2,512,128]{3,2,1,0:T(8,128)(2,1)S(1)}, bf16[2,2,512,128]{3,2,1,0:T(8,128)(2,1)S(1)}, u32[]{:S(2)}, u32[]{:S(2)}) %collective-permute-start.8) | collective-permute-done | bytes 524320 | tf_op jit(solution)/shard_map/ppermute | solution.py:201
  36.2 3.4 %collective-permute-start.13 = (bf16[2,2,512,128]{3,2,1,0:T(8,128)(2,1)S(1)}, bf16[2,2,512,128]{3,2,1,0:T(8,128)(2,1)S(1)}, u32[]{:S(2)}, u32[]{:S(2)}) collective-permute-start(bf16[2,2,512,128]{3,2,1,0:T(8,128)(2,1)S(1)} %get-tuple-element.18), channel_id=1, source_target_pairs={{0,2},{1,3},{6,4},{7,5},{4,6},{5,7},{10,8},{11,9},{8,10},{9,11},{1... | collective-permute-start | bytes 1572872 | tf_op jit(solution)/shard_map/ppermute | solution.py:205
  39.6 0.1 broadcast_select_fusion.1
  39.7 7.7 %collective-permute-done.4.refs_2_ = bf16[2,2,512,128]{3,2,1,0:T(8,128)(2,1)S(1)} collective-permute-done((bf16[2,2,512,128]{3,2,1,0:T(8,128)(2,1)S(1)}, bf16[2,2,512,128]{3,2,1,0:T(8,128)(2,1)S(1)}, u32[]{:S(2)}, u32[]{:S(2)}) %collective-permute-start.4) | collective-permute-done | bytes 524320 | tf_op jit(solution)/shard_map/ppermute | solution.py:201
  47.4 3.4 %collective-permute-start.9 = (bf16[2,2,512,128]{3,2,1,0:T(8,128)(2,1)S(1)}, bf16[2,2,512,128]{3,2,1,0:T(8,128)(2,1)S(1)}, u32[]{:S(2)}, u32[]{:S(2)}) collective-permute-start(bf16[2,2,512,128]{3,2,1,0:T(8,128)(2,1)S(1)} %get-tuple-element.20), channel_id=1, source_target_pairs={{0,2},{1,3},{6,4},{7,5},{4,6},{5,7},{10,8},{11,9},{8,10},{9,11},{1... | collective-permute-start | bytes 1572872 | tf_op jit(solution)/shard_map/ppermute | solution.py:205
  50.9 0.1 broadcast_select_fusion.2
  50.9 1.1 %collective-permute-done.refs_2_ = bf16[1,2,512,128]{3,2,1,0:T(8,128)(2,1)} collective-permute-done((bf16[1,2,512,128]{3,2,1,0:T(8,128)(2,1)}, bf16[1,2,512,128]{3,2,1,0:T(8,128)(2,1)}, u32[]{:S(2)}, u32[]{:S(2)}) %collective-permute-start) | collective-permute-done | bytes 262176 | tf_op jit(solution)/shard_map/ppermute | solution.py:201
  52.0 0.0 collective-permute-start.14
  52.0 0.0 collective-permute-done.17.refs_1_
  52.0 3.4 %collective-permute-start.5 = (bf16[2,2,512,128]{3,2,1,0:T(8,128)(2,1)S(1)}, bf16[2,2,512,128]{3,2,1,0:T(8,128)(2,1)S(1)}, u32[]{:S(2)}, u32[]{:S(2)}) collective-permute-start(bf16[2,2,512,128]{3,2,1,0:T(8,128)(2,1)S(1)} %get-tuple-element.22), channel_id=1, source_target_pairs={{0,2},{1,3},{6,4},{7,5},{4,6},{5,7},{10,8},{11,9},{8,10},{9,11},{1... | collective-permute-start | bytes 1572872 | tf_op jit(solution)/shard_map/ppermute | solution.py:205
  55.5 0.0 collective-permute-done.13.refs_1_
  55.5 0.3 collective-permute-start.15
  55.8 0.0 collective-permute-done.18.refs_3_
  55.8 0.3 collective-permute-start.19
  56.1 0.0 copy-done
  56.1 0.0 copy-done.1
  56.1 1.5 %plan.1 = (bf16[4,1024,128]{2,1,0:T(8,128)(2,1)S(1)}, s32[32]{0:T(128)S(1)}) custom-call(s32[1]{0:T(128)} %bitcast.place, s32[4,8]{1,0:T(4,128)S(1)} %copy-done, s32[4,128]{1,0:T(4,128)S(1)} %bitcast.2), custom_call_target="tpu_custom_call" | custom-call | tf_op jit(solution)/shard_map/plan/pallas_call | solution.py:150
  57.6 1.1 %broadcast_select_fusion.7 = (bf16[1,2,512,128]{3,2,1,0:T(8,128)(2,1)S(1)}, bf16[1,2,512,128]{3,2,1,0:T(8,128)(2,1)S(1)}) fusion(bf16[1,2,512,128]{3,2,1,0:T(8,128)(2,1)} %get-tuple-element.13.refs_0_, bf16[1,2,512,128]{3,2,1,0:T(8,128)(2,1)} %collective-permute-done.refs_2_, pred[]{:T(512)S(6)} %eq.8, pred[]{:T(512)S(6)} %eq.7), kind=kLoop, calls=%fused_computation.7 | loop fusion | flops 262144 | bytes 1048578 | tf_op jit(solution)/shard_map/jit(_where)/select_n | solution.py:206
  58.7 0.0 collective-permute-done.19.refs_4_
  58.7 0.3 collective-permute-start.10
  59.0 5.2 %collective-permute-done.9.refs_1_ = bf16[2,2,512,128]{3,2,1,0:T(8,128)(2,1)S(1)} collective-permute-done((bf16[2,2,512,128]{3,2,1,0:T(8,128)(2,1)S(1)}, bf16[2,2,512,128]{3,2,1,0:T(8,128)(2,1)S(1)}, u32[]{:S(2)}, u32[]{:S(2)}) %collective-permute-start.9) | collective-permute-done | bytes 524320 | tf_op jit(solution)/shard_map/ppermute | solution.py:205
  64.1 0.0 collective-permute-start.11
  64.1 5.5 %attend.5.refs_5_ = bf16[512,4096]{1,0:T(8,128)(2,1)} custom-call(s32[32]{0:T(128)S(1)} %get-tuple-element.11.table, bf16[4,1024,128]{2,1,0:T(8,128)(2,1)S(1)} %get-tuple-element.12.bias, bf16[512,4096]{1,0:T(8,128)(2,1)} %queries.9, bf16[1,2,512,128]{3,2,1,0:T(8,128)(2,1)S(1)} %pack.3.refs_0_, bf16[1,2,512,128]{3,2,1,0:T(8,128)(2,1)S(1)} %collective-permute-done.17.refs_1_, ...), custom_call_target="tpu_custom_call" | custom-call | flops 2147483648 | bytes 8388608 | tf_op jit(solution)/shard_map/attend/pallas_call | solution.py:96
  69.7 0.0 collective-permute-done.14.refs_3_
  69.7 3.6 %collective-permute-start.1 = (bf16[1,2,512,128]{3,2,1,0:T(8,128)(2,1)S(1)}, bf16[1,2,512,128]{3,2,1,0:T(8,128)(2,1)S(1)}, u32[]{:S(2)}, u32[]{:S(2)}) collective-permute-start(bf16[1,2,512,128]{3,2,1,0:T(8,128)(2,1)S(1)} %get-tuple-element.26), channel_id=1, source_target_pairs={{0,2},{1,3},{6,4},{7,5},{4,6},{5,7},{10,8},{11,9},{8,10},{9,11},{1... | collective-permute-start | bytes 786440 | tf_op jit(solution)/shard_map/ppermute | solution.py:205
  73.3 0.0 collective-permute-done.5.refs_1_
  73.3 0.3 collective-permute-start.6
  73.6 0.0 collective-permute-done.15.refs_4_
  73.6 0.3 collective-permute-start.7
  73.9 8.6 %attend.6.refs_5_ = bf16[512,4096]{1,0:T(8,128)(2,1)} custom-call(s32[32]{0:T(128)S(1)} %get-tuple-element.11.table, bf16[4,1024,128]{2,1,0:T(8,128)(2,1)S(1)} %get-tuple-element.12.bias, bf16[512,4096]{1,0:T(8,128)(2,1)} %queries.9, bf16[2,2,512,128]{3,2,1,0:T(8,128)(2,1)S(1)} %get-tuple-element.16.refs_0_, ...), custom_call_target="tpu_custom_call", output_to_operand_aliasing={{}: (8, {})} | custom-call | flops 4294967296 | bytes 8388608 | tf_op jit(solution)/shard_map/attend/pallas_call | solution.py:96
  82.4 0.0 collective-permute-done.1.refs_1_
  82.4 0.2 collective-permute-start.2
  82.6 0.0 collective-permute-done.10.refs_3_
  82.7 0.3 collective-permute-start.3
  83.0 0.0 collective-permute-done.11.refs_4_
  83.0 8.6 %attend.7.refs_5_ = bf16[512,4096]{1,0:T(8,128)(2,1)} custom-call(s32[32]{0:T(128)S(1)} %get-tuple-element.11.table, bf16[4,1024,128]{2,1,0:T(8,128)(2,1)S(1)} %get-tuple-element.12.bias, bf16[512,4096]{1,0:T(8,128)(2,1)} %queries.9, bf16[2,2,512,128]{3,2,1,0:T(8,128)(2,1)S(1)} %get-tuple-element.15.refs_0_, ...), custom_call_target="tpu_custom_call", output_to_operand_aliasing={{}: (8, {})} | custom-call | flops 4294967296 | bytes 8388608 | tf_op jit(solution)/shard_map/attend/pallas_call | solution.py:96
  91.5 0.0 collective-permute-done.6.refs_3_
  91.5 0.0 collective-permute-done.7.refs_4_
  91.5 8.6 %attend.8.refs_5_ = bf16[512,4096]{1,0:T(8,128)(2,1)} custom-call(s32[32]{0:T(128)S(1)} %get-tuple-element.11.table, bf16[4,1024,128]{2,1,0:T(8,128)(2,1)S(1)} %get-tuple-element.12.bias, bf16[512,4096]{1,0:T(8,128)(2,1)} %queries.9, bf16[2,2,512,128]{3,2,1,0:T(8,128)(2,1)S(1)} %get-tuple-element.14.refs_0_, ...), custom_call_target="tpu_custom_call", output_to_operand_aliasing={{}: (8, {})} | custom-call | flops 4294967296 | bytes 8388608 | tf_op jit(solution)/shard_map/attend/pallas_call | solution.py:96
  100.1 0.0 collective-permute-done.2.refs_3_
  100.1 0.0 collective-permute-done.3.refs_4_
  100.1 5.6 %attend.9 = bf16[512,4096]{1,0:T(8,128)(2,1)} custom-call(s32[32]{0:T(128)S(1)} %get-tuple-element.11.table, bf16[4,1024,128]{2,1,0:T(8,128)(2,1)S(1)} %get-tuple-element.12.bias, bf16[512,4096]{1,0:T(8,128)(2,1)} %queries.9, bf16[1,2,512,128]{3,2,1,0:T(8,128)(2,1)} %get-tuple-element.13.refs_0_, ...), custom_call_target="tpu_custom_call", output_to_operand_aliasing={{}: (8, {})} | custom-call | flops 2147483648 | bytes 8388608 | tf_op jit(solution)/shard_map/attend/pallas_call | solution.py:96
Async XLA Ops:
  2.7 26.8 %collective-permute-start.12 = (bf16[2,2,512,128]{3,2,1,0:T(8,128)(2,1)S(1)}, bf16[2,2,512,128]{3,2,1,0:T(8,128)(2,1)S(1)}, u32[]{:S(2)}, u32[]{:S(2)}) collective-permute-start(bf16[2,2,512,128]{3,2,1,0:T(8,128)(2,1)S(1)} %get-tuple-element.16.refs_0_), channel_id=1, source_target_pairs={{0,4},{1,5},{2,6},{3,7},{4,8},{5,9},{6,10},{7,11},{8,12},{9,13},{1... | collective-permute-start | bytes 1572872 | tf_op jit(solution)/shard_map/ppermute | solution.py:201
  5.0 51.0 %copy-start = (s32[4,8]{1,0:T(4,128)S(1)}, s32[4,8]{1,0:T(4,128)}, u32[]{:S(2)}) copy-start(s32[4,8]{1,0:T(4,128)} %listed.1) | copy-start | bytes 388
  5.1 51.0 %copy-start.1 = (s32[512]{0:T(512)S(1)}, s32[512]{0:T(512)}, u32[]{:S(2)}) copy-start(s32[512]{0:T(512)} %param.8) | copy-start | bytes 6148
  5.1 20.0 %collective-permute-start.16 = (bf16[1,2,512,128]{3,2,1,0:T(8,128)(2,1)S(1)}, bf16[1,2,512,128]{3,2,1,0:T(8,128)(2,1)}, u32[]{:S(2)}, u32[]{:S(2)}) collective-permute-start(bf16[1,2,512,128]{3,2,1,0:T(8,128)(2,1)S(1)} %pack.3.refs_0_), channel_id=1, source_target_pairs={{0,4},{1,5},{2,6},{3,7},{4,8},{5,9},{6,10},{7,11},{8,12},{9,13},{1... | collective-permute-start | bytes 786440 | tf_op jit(solution)/shard_map/ppermute | solution.py:201
  6.4 29.8 %collective-permute-start.8 = (bf16[2,2,512,128]{3,2,1,0:T(8,128)(2,1)S(1)}, bf16[2,2,512,128]{3,2,1,0:T(8,128)(2,1)S(1)}, u32[]{:S(2)}, u32[]{:S(2)}) collective-permute-start(bf16[2,2,512,128]{3,2,1,0:T(8,128)(2,1)S(1)} %get-tuple-element.15.refs_0_), channel_id=1, source_target_pairs={{0,4},{1,5},{2,6},{3,7},{4,8},{5,9},{6,10},{7,11},{8,12},{9,13},{1... | collective-permute-start | bytes 1572872 | tf_op jit(solution)/shard_map/ppermute | solution.py:201
  7.7 39.8 %collective-permute-start.4 = (bf16[2,2,512,128]{3,2,1,0:T(8,128)(2,1)S(1)}, bf16[2,2,512,128]{3,2,1,0:T(8,128)(2,1)S(1)}, u32[]{:S(2)}, u32[]{:S(2)}) collective-permute-start(bf16[2,2,512,128]{3,2,1,0:T(8,128)(2,1)S(1)} %get-tuple-element.14.refs_0_), channel_id=1, source_target_pairs={{0,4},{1,5},{2,6},{3,7},{4,8},{5,9},{6,10},{7,11},{8,12},{9,13},{1... | collective-permute-start | bytes 1572872 | tf_op jit(solution)/shard_map/ppermute | solution.py:201
  9.0 43.1 %collective-permute-start = (bf16[1,2,512,128]{3,2,1,0:T(8,128)(2,1)}, bf16[1,2,512,128]{3,2,1,0:T(8,128)(2,1)}, u32[]{:S(2)}, u32[]{:S(2)}) collective-permute-start(bf16[1,2,512,128]{3,2,1,0:T(8,128)(2,1)} %get-tuple-element.13.refs_0_), channel_id=1, source_target_pairs={{0,4},{1,5},{2,6},{3,7},{4,8},{5,9},{6,10},{7,11},{8,12},{9,13},{1... | collective-permute-start | bytes 786440 | tf_op jit(solution)/shard_map/ppermute | solution.py:201
  26.1 26.0 %collective-permute-start.17 = (bf16[1,2,512,128]{3,2,1,0:T(8,128)(2,1)S(1)}, bf16[1,2,512,128]{3,2,1,0:T(8,128)(2,1)S(1)}, u32[]{:S(2)}, u32[]{:S(2)}) collective-permute-start(bf16[1,2,512,128]{3,2,1,0:T(8,128)(2,1)S(1)} %get-tuple-element.24), channel_id=1, source_target_pairs={{0,2},{1,3},{6,4},{7,5},{4,6},{5,7},{10,8},{11,9},{8,10},{9,11},{1... | collective-permute-start | bytes 786440 | tf_op jit(solution)/shard_map/ppermute | solution.py:205
  29.5 26.3 %collective-permute-start.18 = (bf16[1,2,512,128]{3,2,1,0:T(8,128)(2,1)S(1)}, bf16[1,2,512,128]{3,2,1,0:T(8,128)(2,1)S(1)}, u32[]{:S(2)}, u32[]{:S(2)}) collective-permute-start(bf16[1,2,512,128]{3,2,1,0:T(8,128)(2,1)S(1)} %get-tuple-element.23), channel_id=1, source_target_pairs={{1,0},{0,1},{3,2},{2,3},{5,4},{4,5},{7,6},{6,7},{9,8},{8,9},{11,10... | collective-permute-start | bytes 786440 | tf_op jit(solution)/shard_map/ppermute | solution.py:206
  36.2 19.3 %collective-permute-start.13 = (bf16[2,2,512,128]{3,2,1,0:T(8,128)(2,1)S(1)}, bf16[2,2,512,128]{3,2,1,0:T(8,128)(2,1)S(1)}, u32[]{:S(2)}, u32[]{:S(2)}) collective-permute-start(bf16[2,2,512,128]{3,2,1,0:T(8,128)(2,1)S(1)} %get-tuple-element.18), channel_id=1, source_target_pairs={{0,2},{1,3},{6,4},{7,5},{4,6},{5,7},{10,8},{11,9},{8,10},{9,11},{1... | collective-permute-start | bytes 1572872 | tf_op jit(solution)/shard_map/ppermute | solution.py:205
  47.4 16.7 %collective-permute-start.9 = (bf16[2,2,512,128]{3,2,1,0:T(8,128)(2,1)S(1)}, bf16[2,2,512,128]{3,2,1,0:T(8,128)(2,1)S(1)}, u32[]{:S(2)}, u32[]{:S(2)}) collective-permute-start(bf16[2,2,512,128]{3,2,1,0:T(8,128)(2,1)S(1)} %get-tuple-element.20), channel_id=1, source_target_pairs={{0,2},{1,3},{6,4},{7,5},{4,6},{5,7},{10,8},{11,9},{8,10},{9,11},{1... | collective-permute-start | bytes 1572872 | tf_op jit(solution)/shard_map/ppermute | solution.py:205
  52.0 17.6 %collective-permute-start.14 = (bf16[2,2,512,128]{3,2,1,0:T(8,128)(2,1)S(1)}, bf16[2,2,512,128]{3,2,1,0:T(8,128)(2,1)S(1)}, u32[]{:S(2)}, u32[]{:S(2)}) collective-permute-start(bf16[2,2,512,128]{3,2,1,0:T(8,128)(2,1)S(1)} %get-tuple-element.17), channel_id=1, source_target_pairs={{1,0},{0,1},{3,2},{2,3},{5,4},{4,5},{7,6},{6,7},{9,8},{8,9},{11,10... | collective-permute-start | bytes 1572872 | tf_op jit(solution)/shard_map/ppermute | solution.py:206
  52.0 21.2 %collective-permute-start.5 = (bf16[2,2,512,128]{3,2,1,0:T(8,128)(2,1)S(1)}, bf16[2,2,512,128]{3,2,1,0:T(8,128)(2,1)S(1)}, u32[]{:S(2)}, u32[]{:S(2)}) collective-permute-start(bf16[2,2,512,128]{3,2,1,0:T(8,128)(2,1)S(1)} %get-tuple-element.22), channel_id=1, source_target_pairs={{0,2},{1,3},{6,4},{7,5},{4,6},{5,7},{10,8},{11,9},{8,10},{9,11},{1... | collective-permute-start | bytes 1572872 | tf_op jit(solution)/shard_map/ppermute | solution.py:205
  55.5 18.1 %collective-permute-start.15 = (bf16[2,2,512,128]{3,2,1,0:T(8,128)(2,1)S(1)}, bf16[2,2,512,128]{3,2,1,0:T(8,128)(2,1)S(1)}, u32[]{:S(2)}, u32[]{:S(2)}) collective-permute-start(bf16[2,2,512,128]{3,2,1,0:T(8,128)(2,1)S(1)} %collective-permute-done.13.refs_1_), channel_id=1, source_target_pairs={{1,0},{0,1},{3,2},{2,3},{5,4},{4,5},{7,6},{6,7},{9,8},{8,9},{11,10... | collective-permute-start | bytes 1572872 | tf_op jit(solution)/shard_map/ppermute | solution.py:207
  55.8 2.9 %collective-permute-start.19 = (bf16[1,2,512,128]{3,2,1,0:T(8,128)(2,1)S(1)}, bf16[1,2,512,128]{3,2,1,0:T(8,128)(2,1)S(1)}, u32[]{:S(2)}, u32[]{:S(2)}) collective-permute-start(bf16[1,2,512,128]{3,2,1,0:T(8,128)(2,1)S(1)} %collective-permute-done.17.refs_1_), channel_id=1, source_target_pairs={{1,0},{0,1},{3,2},{2,3},{5,4},{4,5},{7,6},{6,7},{9,8},{8,9},{11,10... | collective-permute-start | bytes 786440 | tf_op jit(solution)/shard_map/ppermute | solution.py:207
  58.7 24.0 %collective-permute-start.10 = (bf16[2,2,512,128]{3,2,1,0:T(8,128)(2,1)S(1)}, bf16[2,2,512,128]{3,2,1,0:T(8,128)(2,1)S(1)}, u32[]{:S(2)}, u32[]{:S(2)}) collective-permute-start(bf16[2,2,512,128]{3,2,1,0:T(8,128)(2,1)S(1)} %get-tuple-element.19), channel_id=1, source_target_pairs={{1,0},{0,1},{3,2},{2,3},{5,4},{4,5},{7,6},{6,7},{9,8},{8,9},{11,10... | collective-permute-start | bytes 1572872 | tf_op jit(solution)/shard_map/ppermute | solution.py:206
  64.1 18.8 %collective-permute-start.11 = (bf16[2,2,512,128]{3,2,1,0:T(8,128)(2,1)S(1)}, bf16[2,2,512,128]{3,2,1,0:T(8,128)(2,1)S(1)}, u32[]{:S(2)}, u32[]{:S(2)}) collective-permute-start(bf16[2,2,512,128]{3,2,1,0:T(8,128)(2,1)S(1)} %collective-permute-done.9.refs_1_), channel_id=1, source_target_pairs={{1,0},{0,1},{3,2},{2,3},{5,4},{4,5},{7,6},{6,7},{9,8},{8,9},{11,10... | collective-permute-start | bytes 1572872 | tf_op jit(solution)/shard_map/ppermute | solution.py:207
  69.7 12.8 %collective-permute-start.1 = (bf16[1,2,512,128]{3,2,1,0:T(8,128)(2,1)S(1)}, bf16[1,2,512,128]{3,2,1,0:T(8,128)(2,1)S(1)}, u32[]{:S(2)}, u32[]{:S(2)}) collective-permute-start(bf16[1,2,512,128]{3,2,1,0:T(8,128)(2,1)S(1)} %get-tuple-element.26), channel_id=1, source_target_pairs={{0,2},{1,3},{6,4},{7,5},{4,6},{5,7},{10,8},{11,9},{8,10},{9,11},{1... | collective-permute-start | bytes 786440 | tf_op jit(solution)/shard_map/ppermute | solution.py:205
  73.3 18.2 %collective-permute-start.6 = (bf16[2,2,512,128]{3,2,1,0:T(8,128)(2,1)S(1)}, bf16[2,2,512,128]{3,2,1,0:T(8,128)(2,1)S(1)}, u32[]{:S(2)}, u32[]{:S(2)}) collective-permute-start(bf16[2,2,512,128]{3,2,1,0:T(8,128)(2,1)S(1)} %get-tuple-element.21), channel_id=1, source_target_pairs={{1,0},{0,1},{3,2},{2,3},{5,4},{4,5},{7,6},{6,7},{9,8},{8,9},{11,10... | collective-permute-start | bytes 1572872 | tf_op jit(solution)/shard_map/ppermute | solution.py:206
  73.6 18.0 %collective-permute-start.7 = (bf16[2,2,512,128]{3,2,1,0:T(8,128)(2,1)S(1)}, bf16[2,2,512,128]{3,2,1,0:T(8,128)(2,1)S(1)}, u32[]{:S(2)}, u32[]{:S(2)}) collective-permute-start(bf16[2,2,512,128]{3,2,1,0:T(8,128)(2,1)S(1)} %collective-permute-done.5.refs_1_), channel_id=1, source_target_pairs={{1,0},{0,1},{3,2},{2,3},{5,4},{4,5},{7,6},{6,7},{9,8},{8,9},{11,10... | collective-permute-start | bytes 1572872 | tf_op jit(solution)/shard_map/ppermute | solution.py:207
  82.4 17.7 %collective-permute-start.2 = (bf16[1,2,512,128]{3,2,1,0:T(8,128)(2,1)S(1)}, bf16[1,2,512,128]{3,2,1,0:T(8,128)(2,1)S(1)}, u32[]{:S(2)}, u32[]{:S(2)}) collective-permute-start(bf16[1,2,512,128]{3,2,1,0:T(8,128)(2,1)S(1)} %get-tuple-element.25), channel_id=1, source_target_pairs={{1,0},{0,1},{3,2},{2,3},{5,4},{4,5},{7,6},{6,7},{9,8},{8,9},{11,10... | collective-permute-start | bytes 786440 | tf_op jit(solution)/shard_map/ppermute | solution.py:206
  82.7 17.5 %collective-permute-start.3 = (bf16[1,2,512,128]{3,2,1,0:T(8,128)(2,1)S(1)}, bf16[1,2,512,128]{3,2,1,0:T(8,128)(2,1)S(1)}, u32[]{:S(2)}, u32[]{:S(2)}) collective-permute-start(bf16[1,2,512,128]{3,2,1,0:T(8,128)(2,1)S(1)} %collective-permute-done.1.refs_1_), channel_id=1, source_target_pairs={{1,0},{0,1},{3,2},{2,3},{5,4},{4,5},{7,6},{6,7},{9,8},{8,9},{11,10... | collective-permute-start | bytes 786440 | tf_op jit(solution)/shard_map/ppermute | solution.py:207

commit v3 on v2

--- a/solution.py
+++ b/solution.py
@@ -21,9 +21,9 @@
 SCALE = HEAD_DIM**-0.5 * LOG2E
 
 
-def kernel(aliased, table, bias, queries, *refs):
-    sources = refs[:SHARDS]
-    out, key_window, value_window, scores, weights, tops = refs[SHARDS + aliased :]
+def kernel(first, earlier, table, bias, queries, *refs):
+    sources, done = refs[:SHARDS], refs[SHARDS : SHARDS + len(earlier)]
+    out, key_window, value_window, scores, weights, tops, *rest = refs[SHARDS + len(earlier) :]
     step = pl.program_id(0)
     blocks, listed = bias.shape[0], bias.shape[1]
     slots = listed // BLOCK
@@ -33,6 +33,29 @@
         for n, source in enumerate(sources):
             window[n * shard_rows : (n + 1) * shard_rows, :] = source[step, m]
 
+    def columns_of(head):
+        return pl.ds(pl.multiple_of(head * width, width), width)
+
+    staged, moves = out, []
+    if earlier:
+        staged, early_sems, own_sems = rest
+        for n, (start, part) in enumerate(zip(earlier, done)):
+            columns = slice(start * width, start * width + part.shape[1])
+            moves.append(pltpu.make_async_copy(part, out.at[:, columns], early_sems.at[n]))
+
+        @pl.when(step == 0)
+        def _():
+            for move in moves:
+                move.start()
+
+    def own_move(block_id):
+        rows = pl.ds(block_id * BLOCK, BLOCK)
+        return pltpu.make_async_copy(
+            staged.at[rows, columns_of(step)],
+            out.at[rows, columns_of(first + step)],
+            own_sems.at[step, block_id],
+        )
+
     row_ids = lax.broadcasted_iota(jnp.int32, (BLOCK, BLOCK), 0)
     column_ids = lax.broadcasted_iota(jnp.int32, (BLOCK, BLOCK), 1)
     eye = (row_ids == column_ids).astype(jnp.bfloat16)
@@ -48,7 +71,10 @@
 
     def score(block_id, b):
         rows = slice(block_id * BLOCK, (block_id + 1) * BLOCK)
-        stacked = [queries[rows, h * HEAD_DIM : (h + 1) * HEAD_DIM] for h in range(GROUP)]
+        stacked = []
+        for h in range(GROUP):
+            column = pl.multiple_of((first + step) * width + h * HEAD_DIM, HEAD_DIM)
+            stacked.append(queries[rows, pl.ds(column, HEAD_DIM)])
         found = lax.dot_general(
             jnp.concatenate([jnp.concatenate(parts(key_window, block_id), 0), bias[block_id]], 1),
             jnp.concatenate([jnp.concatenate(stacked, 0), picker], 1),
@@ -73,8 +99,8 @@
         result = mixed[:HEAD_DIM] * (1.0 / mixed[HEAD_DIM : HEAD_DIM + 1])
         rows = slice(block_id * BLOCK, (block_id + 1) * BLOCK)
         for h in range(GROUP):
-            columns = slice(h * HEAD_DIM, (h + 1) * HEAD_DIM)
-            out[rows, columns] = result[:, h * BLOCK : (h + 1) * BLOCK].T.astype(jnp.bfloat16)
+            columns = pl.ds(pl.multiple_of(step * width + h * HEAD_DIM, HEAD_DIM), HEAD_DIM)
+            staged[rows, columns] = result[:, h * BLOCK : (h + 1) * BLOCK].T.astype(jnp.bfloat16)
 
     for t in range(blocks + 2):
         if t < blocks:
@@ -83,42 +109,60 @@
             soften((t - 1) % 2)
         if 0 <= t - 2 < blocks:
             mix(t - 2, (t - 2) % 2)
-
-
-def attend(table, bias, queries, sources, previous, first, heads):
+            if earlier:
+                own_move(t - 2).start()
+    if earlier:
+        for b in range(blocks):
+            own_move(b).wait()
+
+        @pl.when(step + 1 == pl.num_programs(0))
+        def _():
+            for move in moves:
+                move.wait()
+
+
+def attend(table, bias, queries, sources, earlier, first, heads):
     tokens, width = queries.shape
-    listed = bias.shape[1]
+    blocks, listed = bias.shape[0], bias.shape[1]
     group_width = GROUP * HEAD_DIM
-    aliased = 0 if previous is None else 1
     near = pl.BlockSpec(memory_space=pltpu.VMEM)
-    columns = pl.BlockSpec((tokens, group_width), lambda i, t: (0, first + i))
     work = tokens * GROUP * heads * listed * HEAD_DIM
+    scratch = [
+        pltpu.VMEM((SHARDS * tokens, HEAD_DIM), jnp.bfloat16),
+        pltpu.VMEM((SHARDS * tokens, HEAD_DIM), jnp.bfloat16),
+        pltpu.VMEM((2, listed, group_width), jnp.float32),
+        pltpu.VMEM((2, listed, group_width), jnp.bfloat16),
+        pltpu.VMEM((2, 8, group_width), jnp.float32),
+    ]
+    if earlier:
+        scratch += [
+            pltpu.VMEM((tokens, heads * group_width), jnp.bfloat16),
+            pltpu.SemaphoreType.DMA((len(earlier),)),
+            pltpu.SemaphoreType.DMA((heads, blocks)),
+        ]
+    else:
+        width = heads * group_width
     return pl.pallas_call(
-        functools.partial(kernel, aliased),
+        functools.partial(kernel, first, tuple(start for start, _ in earlier)),
         grid_spec=pltpu.PrefetchScalarGridSpec(
             num_scalar_prefetch=1,
             grid=(heads,),
-            in_specs=[near, columns] + [near] * SHARDS + [pl.BlockSpec(memory_space=pl.ANY)] * aliased,
-            out_specs=columns,
-            scratch_shapes=[
-                pltpu.VMEM((SHARDS * tokens, HEAD_DIM), jnp.bfloat16),
-                pltpu.VMEM((SHARDS * tokens, HEAD_DIM), jnp.bfloat16),
-                pltpu.VMEM((2, listed, group_width), jnp.float32),
-                pltpu.VMEM((2, listed, group_width), jnp.bfloat16),
-                pltpu.VMEM((2, 8, group_width), jnp.float32),
-            ],
+            in_specs=[near] * (2 + SHARDS + len(earlier)),
+            out_specs=pl.BlockSpec(memory_space=pltpu.HBM) if earlier else near,
+            scratch_shapes=scratch,
         ),
         out_shape=jax.ShapeDtypeStruct((tokens, width), jnp.bfloat16),
-        input_output_aliases={3 + SHARDS: 0} if aliased else {},
         cost_estimate=pl.CostEstimate(
             flops=8 * work, bytes_accessed=4 * tokens * width, transcendentals=work // HEAD_DIM
         ),
         compiler_params=pltpu.CompilerParams(vmem_limit_bytes=VMEM_LIMIT),
         name="attend",
-    )(table, bias, pltpu.with_memory_space_constraint(queries, pltpu.HBM), *sources, *(() if previous is None else (previous,)))
-
-
-def plan_kernel(place, listed, starts, bias, table):
+    )(table, bias, queries, *sources, *(part for _, part in earlier))
+
+
+def plan_kernel(place, listed, starts, queries, bias, table, near_queries, sem):
+    fetch = pltpu.make_async_copy(queries, near_queries, sem)
+    fetch.start()
     shard = place[0]
     blocks, slots = listed.shape
     core = shard % 2
@@ -142,22 +186,25 @@
             where = jnp.where(behind == 4, 2, where)
             where = jnp.where(entry >= 0, where, 0)
             table[b * slots + j] = where * blocks + known - shard_of * blocks
-
-
-def plan(doc_start, block_list, shard):
+    fetch.wait()
+
+
+def plan(doc_start, block_list, queries, shard):
     blocks, slots = block_list.shape
     scalars, vectors = pl.BlockSpec(memory_space=pltpu.SMEM), pl.BlockSpec(memory_space=pltpu.VMEM)
     return pl.pallas_call(
         plan_kernel,
-        in_specs=[scalars, scalars, vectors],
-        out_specs=[vectors, scalars],
+        in_specs=[scalars, scalars, vectors, pl.BlockSpec(memory_space=pltpu.HBM)],
+        out_specs=[vectors, scalars, vectors],
         out_shape=[
             jax.ShapeDtypeStruct((blocks, slots * BLOCK, BLOCK), jnp.bfloat16),
             jax.ShapeDtypeStruct((blocks * slots,), jnp.int32),
+            jax.ShapeDtypeStruct(queries.shape, queries.dtype),
         ],
+        scratch_shapes=[pltpu.SemaphoreType.DMA],
         compiler_params=pltpu.CompilerParams(vmem_limit_bytes=VMEM_LIMIT),
         name="plan",
-    )(shard.reshape(1), block_list, doc_start.reshape(blocks, BLOCK))
+    )(shard.reshape(1), block_list, doc_start.reshape(blocks, BLOCK), pltpu.with_memory_space_constraint(queries, pltpu.HBM))
 
 
 def pack_kernel(spans, keys, values, *outs):
@@ -192,21 +239,23 @@
     two_back = [(i - 4, i) for i in devices if i >= 4]
     one_back = [(i ^ 2, i) for i in devices if i >= 2]
     sibling = [(i ^ 1, i) for i in devices]
-    bias, table = plan(doc_start, block_list, shard)
+    bias, table, queries = plan(doc_start, block_list, queries, shard)
     firsts = [sum(CHUNKS[:n]) for n in range(len(CHUNKS))]
     spans = list(zip(firsts, CHUNKS))
     owns = pack(keys, values, spans[:1]) + pack(keys, values, spans[1:])
     from_z = []
     for n in range(len(CHUNKS)):
         from_z.append(lax.ppermute(owns[n], "seq", two_back))
-    out = None
+    parts = []
     for n, heads in enumerate(CHUNKS):
         own, back = owns[n], from_z[n]
         from_y = lax.ppermute(jnp.where(row == 0, own, back), "seq", one_back)
         twin_x = lax.ppermute(jnp.where(core == 0, own, back), "seq", sibling)
         twin_y = lax.ppermute(from_y, "seq", sibling)
-        out = attend(table, bias, queries, (own, from_y, back, twin_x, twin_y), out, firsts[n], heads)
-    return out
+        sources = (own, from_y, back, twin_x, twin_y)
+        earlier = parts if n + 1 == len(CHUNKS) else []
+        parts.append((firsts[n], attend(table, bias, queries, sources, earlier, firsts[n], heads)))
+    return parts[-1][1]
 
 
 def solution(mesh):

time: 107 us -> 101 us (0.944)
  Pallas kernels: 42.1 us -> 37.7 us
  waiting for transfers between devices: 35.3 us -> 33.5 us
    pallas_call x6, Pallas kernels: 38.4 us -> 34.7 us  [the longest x5 31.3 us: attend(): pl.pallas_call(functools.partial(kernel, first, tuple((start for start, _...]
    ppermute x5, waiting for transfers between devices: 30.1 us -> 29 us  [routed(): from_z.append(lax.ppermute(owns[n], 'seq', two_back))]
  transfers between devices with their start and end apart: 20 -> 20, of which waited for: 5 -> 5; matrix products, arithmetic and copies ran while one was open for 2% -> 2% of each run, Pallas kernels for 32% -> 30%
where the time goes in v3:
time: 101 us; the launch traced here: 99.8 us
  Pallas kernels  37.7 us (37%)
  waiting for transfers between devices  33.5 us (33%)
  starting transfers between devices  25.8 us (26%)
  other arithmetic  2.29 us (2%)
    pallas_call x5, Pallas kernels, attend(): pl.pallas_call(functools.partial(kernel, first, tuple((start for start, _...  31.3 us
    ppermute x5, waiting for transfers between devices, routed(): from_z.append(lax.ppermute(owns[n], 'seq', two_back))  29 us
    ppermute x5, starting transfers between devices, routed(): from_y = lax.ppermute(jnp.where(row == 0, own, back), 'seq', one_back)  17.3 us
    ppermute x5, starting transfers between devices, routed(): from_z.append(lax.ppermute(owns[n], 'seq', two_back))  6.46 us
    ppermute x5, waiting for transfers between devices, routed(): from_y = lax.ppermute(jnp.where(row == 0, own, back), 'seq', one_back)  4.46 us
    pallas_call x1, Pallas kernels, plan(): pl.pallas_call(plan_kernel, in_specs=[scalars, scalars, vectors, pl.Block...  3.35 us
    pallas_call x2, Pallas kernels, pack(): pl.pallas_call(functools.partial(pack_kernel, spans), grid=(1,), in_specs...  3.04 us
    select_n x5, other arithmetic, routed(): twin_x = lax.ppermute(jnp.where(core == 0, own, back), 'seq', sibling)  2.29 us
  transfers between devices with their start and end apart: 20, of which 5 were waited for; matrix products, arithmetic and copies ran while one was open for 2% of the time, Pallas kernels for 30%

profile of v3, /device:TPU:24, one launch (start us, length us, event | category | flops | bytes accessed | tf_op | source)
XLA Modules:
  0.0 99.8 jit_solution(5682186172509634630)
XLA Ops:
  0.0 2.0 %pack.2 = (bf16[2,2,512,128]{3,2,1,0:T(8,128)(2,1)S(1)}, bf16[2,2,512,128]{3,2,1,0:T(8,128)(2,1)S(1)}, bf16[2,2,512,128]{3,2,1,0:T(8,128)(2,1)S(1)}, bf16[1,2,512,128]{3,2,1,0:T(8,128)(2,1)S(1)}) custom-call(bf16[512,1024]{1,0:T(8,128)(2,1)} %keys.3, bf16[512,1024]{1,0:T(8,128)(2,1)} %values.3), custom_call_target="tpu_custom_call" | custom-call | tf_op jit(solution)/shard_map/pack/pallas_call | solution.py:224
  2.0 1.3 %collective-permute-start.16 = (bf16[2,2,512,128]{3,2,1,0:T(8,128)(2,1)S(1)}, bf16[2,2,512,128]{3,2,1,0:T(8,128)(2,1)}, u32[]{:S(2)}, u32[]{:S(2)}) collective-permute-start(bf16[2,2,512,128]{3,2,1,0:T(8,128)(2,1)S(1)} %get-tuple-element.18.refs_0_), channel_id=1, source_target_pairs={{0,4},{1,5},{2,6},{3,7},{4,8},{5,9},{6,10},{7,11},{8,12},{9,13},{1... | collective-permute-start | bytes 1572872 | tf_op jit(solution)/shard_map/ppermute | solution.py:248
  3.3 1.1 %pack.3.refs_0_ = bf16[1,2,512,128]{3,2,1,0:T(8,128)(2,1)S(1)} custom-call(bf16[512,1024]{1,0:T(8,128)(2,1)} %keys.3, bf16[512,1024]{1,0:T(8,128)(2,1)} %values.3), custom_call_target="tpu_custom_call" | custom-call | tf_op jit(solution)/shard_map/pack/pallas_call | solution.py:224
  4.4 0.0 copy-start
  4.4 0.0 copy-start.1
  4.4 1.3 %collective-permute-start.4 = (bf16[1,2,512,128]{3,2,1,0:T(8,128)(2,1)S(1)}, bf16[1,2,512,128]{3,2,1,0:T(8,128)(2,1)}, u32[]{:S(2)}, u32[]{:S(2)}) collective-permute-start(bf16[1,2,512,128]{3,2,1,0:T(8,128)(2,1)S(1)} %pack.3.refs_0_), channel_id=1, source_target_pairs={{0,4},{1,5},{2,6},{3,7},{4,8},{5,9},{6,10},{7,11},{8,12},{9,13},{1... | collective-permute-start | bytes 786440 | tf_op jit(solution)/shard_map/ppermute | solution.py:248
  5.7 1.3 %collective-permute-start.12 = (bf16[2,2,512,128]{3,2,1,0:T(8,128)(2,1)S(1)}, bf16[2,2,512,128]{3,2,1,0:T(8,128)(2,1)S(1)}, u32[]{:S(2)}, u32[]{:S(2)}) collective-permute-start(bf16[2,2,512,128]{3,2,1,0:T(8,128)(2,1)S(1)} %get-tuple-element.17.refs_0_), channel_id=1, source_target_pairs={{0,4},{1,5},{2,6},{3,7},{4,8},{5,9},{6,10},{7,11},{8,12},{9,13},{1... | collective-permute-start | bytes 1572872 | tf_op jit(solution)/shard_map/ppermute | solution.py:248
  7.0 1.3 %collective-permute-start.8 = (bf16[2,2,512,128]{3,2,1,0:T(8,128)(2,1)S(1)}, bf16[2,2,512,128]{3,2,1,0:T(8,128)(2,1)S(1)}, u32[]{:S(2)}, u32[]{:S(2)}) collective-permute-start(bf16[2,2,512,128]{3,2,1,0:T(8,128)(2,1)S(1)} %get-tuple-element.16.refs_0_), channel_id=1, source_target_pairs={{0,4},{1,5},{2,6},{3,7},{4,8},{5,9},{6,10},{7,11},{8,12},{9,13},{1... | collective-permute-start | bytes 1572872 | tf_op jit(solution)/shard_map/ppermute | solution.py:248
  8.3 1.3 %collective-permute-start = (bf16[1,2,512,128]{3,2,1,0:T(8,128)(2,1)S(1)}, bf16[1,2,512,128]{3,2,1,0:T(8,128)(2,1)S(1)}, u32[]{:S(2)}, u32[]{:S(2)}) collective-permute-start(bf16[1,2,512,128]{3,2,1,0:T(8,128)(2,1)S(1)} %get-tuple-element.15.refs_0_), channel_id=1, source_target_pairs={{0,4},{1,5},{2,6},{3,7},{4,8},{5,9},{6,10},{7,11},{8,12},{9,13},{1... | collective-permute-start | bytes 786440 | tf_op jit(solution)/shard_map/ppermute | solution.py:248
  9.6 14.8 %collective-permute-done.4.refs_2_ = bf16[1,2,512,128]{3,2,1,0:T(8,128)(2,1)} collective-permute-done((bf16[1,2,512,128]{3,2,1,0:T(8,128)(2,1)S(1)}, bf16[1,2,512,128]{3,2,1,0:T(8,128)(2,1)}, u32[]{:S(2)}, u32[]{:S(2)}) %collective-permute-start.4) | collective-permute-done | bytes 262176 | tf_op jit(solution)/shard_map/ppermute | solution.py:248
  24.4 1.0 broadcast_select_fusion.6
  25.4 3.4 %collective-permute-start.5 = (bf16[1,2,512,128]{3,2,1,0:T(8,128)(2,1)S(1)}, bf16[1,2,512,128]{3,2,1,0:T(8,128)(2,1)S(1)}, u32[]{:S(2)}, u32[]{:S(2)}) collective-permute-start(bf16[1,2,512,128]{3,2,1,0:T(8,128)(2,1)S(1)} %get-tuple-element.26), channel_id=1, source_target_pairs={{0,2},{1,3},{6,4},{7,5},{4,6},{5,7},{10,8},{11,9},{8,10},{9,11},{1... | collective-permute-start | bytes 786440 | tf_op jit(solution)/shard_map/ppermute | solution.py:252
  28.8 0.0 collective-permute-done.16.refs_2_
  28.8 0.1 collective-permute-start.6
  28.9 1.1 %broadcast_select_fusion = (bf16[2,2,512,128]{3,2,1,0:T(8,128)(2,1)S(1)}, bf16[2,2,512,128]{3,2,1,0:T(8,128)(2,1)S(1)}) fusion(bf16[2,2,512,128]{3,2,1,0:T(8,128)(2,1)S(1)} %get-tuple-element.18.refs_0_, bf16[2,2,512,128]{3,2,1,0:T(8,128)(2,1)} %collective-permute-done.16.refs_2_, pred[]{:T(512)S(6)} %eq.8, pred[]{:T(512)S(6)} %eq.7), kind=kLoop, calls=%fused_computation | loop fusion | flops 524288 | bytes 2097154 | tf_op jit(solution)/shard_map/jit(_where)/select_n | solution.py:253
  30.0 5.5 %collective-permute-done.12.refs_2_ = bf16[2,2,512,128]{3,2,1,0:T(8,128)(2,1)S(1)} collective-permute-done((bf16[2,2,512,128]{3,2,1,0:T(8,128)(2,1)S(1)}, bf16[2,2,512,128]{3,2,1,0:T(8,128)(2,1)S(1)}, u32[]{:S(2)}, u32[]{:S(2)}) %collective-permute-start.12) | collective-permute-done | bytes 524320 | tf_op jit(solution)/shard_map/ppermute | solution.py:248
  35.5 3.4 %collective-permute-start.17 = (bf16[2,2,512,128]{3,2,1,0:T(8,128)(2,1)S(1)}, bf16[2,2,512,128]{3,2,1,0:T(8,128)(2,1)S(1)}, u32[]{:S(2)}, u32[]{:S(2)}) collective-permute-start(bf16[2,2,512,128]{3,2,1,0:T(8,128)(2,1)S(1)} %get-tuple-element.20), channel_id=1, source_target_pairs={{0,2},{1,3},{6,4},{7,5},{4,6},{5,7},{10,8},{11,9},{8,10},{9,11},{1... | collective-permute-start | bytes 1572872 | tf_op jit(solution)/shard_map/ppermute | solution.py:252
  38.9 0.1 broadcast_select_fusion.1
  39.0 7.7 %collective-permute-done.8.refs_2_ = bf16[2,2,512,128]{3,2,1,0:T(8,128)(2,1)S(1)} collective-permute-done((bf16[2,2,512,128]{3,2,1,0:T(8,128)(2,1)S(1)}, bf16[2,2,512,128]{3,2,1,0:T(8,128)(2,1)S(1)}, u32[]{:S(2)}, u32[]{:S(2)}) %collective-permute-start.8) | collective-permute-done | bytes 524320 | tf_op jit(solution)/shard_map/ppermute | solution.py:248
  46.8 3.4 %collective-permute-start.13 = (bf16[2,2,512,128]{3,2,1,0:T(8,128)(2,1)S(1)}, bf16[2,2,512,128]{3,2,1,0:T(8,128)(2,1)S(1)}, u32[]{:S(2)}, u32[]{:S(2)}) collective-permute-start(bf16[2,2,512,128]{3,2,1,0:T(8,128)(2,1)S(1)} %get-tuple-element.22), channel_id=1, source_target_pairs={{0,2},{1,3},{6,4},{7,5},{4,6},{5,7},{10,8},{11,9},{8,10},{9,11},{1... | collective-permute-start | bytes 1572872 | tf_op jit(solution)/shard_map/ppermute | solution.py:252
  50.2 0.1 broadcast_select_fusion.2
  50.3 1.0 collective-permute-done.refs_2_
  51.2 0.0 collective-permute-start.18
  51.2 0.0 collective-permute-done.5.refs_1_
  51.3 3.4 %collective-permute-start.9 = (bf16[2,2,512,128]{3,2,1,0:T(8,128)(2,1)S(1)}, bf16[2,2,512,128]{3,2,1,0:T(8,128)(2,1)S(1)}, u32[]{:S(2)}, u32[]{:S(2)}) collective-permute-start(bf16[2,2,512,128]{3,2,1,0:T(8,128)(2,1)S(1)} %get-tuple-element.24), channel_id=1, source_target_pairs={{0,2},{1,3},{6,4},{7,5},{4,6},{5,7},{10,8},{11,9},{8,10},{9,11},{1... | collective-permute-start | bytes 1572872 | tf_op jit(solution)/shard_map/ppermute | solution.py:252
  54.7 0.0 collective-permute-done.17.refs_1_
  54.7 0.3 collective-permute-start.19
  55.0 0.0 collective-permute-done.6.refs_3_
  55.0 0.3 collective-permute-start.7
  55.3 0.0 copy-done
  55.3 0.0 copy-done.1
  55.3 3.4 %plan.1 = (bf16[4,1024,128]{2,1,0:T(8,128)(2,1)S(1)}, s32[32]{0:T(128)S(1)}, bf16[512,4096]{1,0:T(8,128)(2,1)S(1)}) custom-call(s32[1]{0:T(128)} %bitcast.place, s32[4,8]{1,0:T(4,128)S(1)} %copy-done, s32[4,128]{1,0:T(4,128)S(1)} %bitcast.2, bf16[512,4096]{1,0:T(8,128)(2,1)} %queries.1), custom_call_target="tpu_custom_call" | custom-call | tf_op jit(solution)/shard_map/plan/pallas_call | solution.py:195
  58.7 0.0 collective-permute-done.7.refs_4_
  58.7 0.3 collective-permute-start.14
  59.0 4.4 %collective-permute-done.13.refs_1_ = bf16[2,2,512,128]{3,2,1,0:T(8,128)(2,1)S(1)} collective-permute-done((bf16[2,2,512,128]{3,2,1,0:T(8,128)(2,1)S(1)}, bf16[2,2,512,128]{3,2,1,0:T(8,128)(2,1)S(1)}, u32[]{:S(2)}, u32[]{:S(2)}) %collective-permute-start.13) | collective-permute-done | bytes 524320 | tf_op jit(solution)/shard_map/ppermute | solution.py:252
  63.4 0.0 collective-permute-start.15
  63.4 4.6 %attend.5.refs_5_ = bf16[512,512]{1,0:T(8,128)(2,1)S(1)} custom-call(s32[32]{0:T(128)S(1)} %get-tuple-element.12.table, bf16[4,1024,128]{2,1,0:T(8,128)(2,1)S(1)} %get-tuple-element.13.bias, bf16[512,4096]{1,0:T(8,128)(2,1)S(1)} %get-tuple-element.14.queries, bf16[1,2,512,128]{3,2,1,0:T(8,128)(2,1)S(1)} %pack.3.refs_0_, ...), custom_call_target="tpu_custom_call" | custom-call | flops 2147483648 | bytes 1048576 | tf_op jit(solution)/shard_map/attend/pallas_call | solution.py:145
  68.0 0.0 collective-permute-done.18.refs_3_
  68.0 3.6 %collective-permute-start.1 = (bf16[1,2,512,128]{3,2,1,0:T(8,128)(2,1)S(1)}, bf16[1,2,512,128]{3,2,1,0:T(8,128)(2,1)S(1)}, u32[]{:S(2)}, u32[]{:S(2)}) collective-permute-start(bf16[1,2,512,128]{3,2,1,0:T(8,128)(2,1)S(1)} %get-tuple-element.28), channel_id=1, source_target_pairs={{0,2},{1,3},{6,4},{7,5},{4,6},{5,7},{10,8},{11,9},{8,10},{9,11},{1... | collective-permute-start | bytes 786440 | tf_op jit(solution)/shard_map/ppermute | solution.py:252
  71.6 0.0 collective-permute-done.9.refs_1_
  71.7 0.3 collective-permute-start.10
  71.9 0.0 collective-permute-done.19.refs_4_
  71.9 0.3 collective-permute-start.11
  72.2 7.8 %attend.8.refs_8_ = bf16[512,1024]{1,0:T(8,128)(2,1)S(1)} custom-call(s32[32]{0:T(128)S(1)} %get-tuple-element.12.table, bf16[4,1024,128]{2,1,0:T(8,128)(2,1)S(1)} %get-tuple-element.13.bias, bf16[512,4096]{1,0:T(8,128)(2,1)S(1)} %get-tuple-element.14.queries, bf16[2,2,512,128]{3,2,1,0:T(8,128)(2,1)S(1)} %get-tuple-element.18.refs_0_, ...), custom_call_target="tpu_custom_call" | custom-call | flops 4294967296 | bytes 2097152 | tf_op jit(solution)/shard_map/attend/pallas_call | solution.py:145
  80.1 0.0 collective-permute-done.1.refs_1_
  80.1 0.3 collective-permute-start.2
  80.4 0.0 collective-permute-done.14.refs_3_
  80.4 0.3 collective-permute-start.3
  80.7 0.0 collective-permute-done.15.refs_4_
  80.7 6.8 %attend.7.refs_7_ = bf16[512,1024]{1,0:T(8,128)(2,1)S(1)} custom-call(s32[32]{0:T(128)S(1)} %get-tuple-element.12.table, bf16[4,1024,128]{2,1,0:T(8,128)(2,1)S(1)} %get-tuple-element.13.bias, bf16[512,4096]{1,0:T(8,128)(2,1)S(1)} %get-tuple-element.14.queries, bf16[2,2,512,128]{3,2,1,0:T(8,128)(2,1)S(1)} %get-tuple-element.17.refs_0_, ...), custom_call_target="tpu_custom_call" | custom-call | flops 4294967296 | bytes 2097152 | tf_op jit(solution)/shard_map/attend/pallas_call | solution.py:145
  87.5 0.0 collective-permute-done.10.refs_3_
  87.5 0.0 collective-permute-done.11.refs_4_
  87.5 6.8 %attend.6.refs_6_ = bf16[512,1024]{1,0:T(8,128)(2,1)S(1)} custom-call(s32[32]{0:T(128)S(1)} %get-tuple-element.12.table, bf16[4,1024,128]{2,1,0:T(8,128)(2,1)S(1)} %get-tuple-element.13.bias, bf16[512,4096]{1,0:T(8,128)(2,1)S(1)} %get-tuple-element.14.queries, bf16[2,2,512,128]{3,2,1,0:T(8,128)(2,1)S(1)} %get-tuple-element.16.refs_0_, ...), custom_call_target="tpu_custom_call" | custom-call | flops 4294967296 | bytes 2097152 | tf_op jit(solution)/shard_map/attend/pallas_call | solution.py:145
  94.3 0.0 collective-permute-done.2.refs_3_
  94.3 0.0 collective-permute-done.3.refs_4_
  94.3 5.3 %attend.9 = bf16[512,4096]{1,0:T(8,128)(2,1)} custom-call(s32[32]{0:T(128)S(1)} %get-tuple-element.12.table, bf16[4,1024,128]{2,1,0:T(8,128)(2,1)S(1)} %get-tuple-element.13.bias, bf16[512,4096]{1,0:T(8,128)(2,1)S(1)} %get-tuple-element.14.queries, bf16[1,2,512,128]{3,2,1,0:T(8,128)(2,1)S(1)} %get-tuple-element.15.refs_0_, ...), custom_call_target="tpu_custom_call" | custom-call | flops 2147483648 | bytes 8388608 | tf_op jit(solution)/shard_map/attend/pallas_call | solution.py:145
  (1 shorter events, 0.0 us)
Async XLA Ops:
  2.0 26.8 %collective-permute-start.16 = (bf16[2,2,512,128]{3,2,1,0:T(8,128)(2,1)S(1)}, bf16[2,2,512,128]{3,2,1,0:T(8,128)(2,1)}, u32[]{:S(2)}, u32[]{:S(2)}) collective-permute-start(bf16[2,2,512,128]{3,2,1,0:T(8,128)(2,1)S(1)} %get-tuple-element.18.refs_0_), channel_id=1, source_target_pairs={{0,4},{1,5},{2,6},{3,7},{4,8},{5,9},{6,10},{7,11},{8,12},{9,13},{1... | collective-permute-start | bytes 1572872 | tf_op jit(solution)/shard_map/ppermute | solution.py:248
  4.4 50.9 %copy-start = (s32[4,8]{1,0:T(4,128)S(1)}, s32[4,8]{1,0:T(4,128)}, u32[]{:S(2)}) copy-start(s32[4,8]{1,0:T(4,128)} %listed.1) | copy-start | bytes 388
  4.4 50.9 %copy-start.1 = (s32[512]{0:T(512)S(1)}, s32[512]{0:T(512)}, u32[]{:S(2)}) copy-start(s32[512]{0:T(512)} %param.8) | copy-start | bytes 6148
  4.4 20.0 %collective-permute-start.4 = (bf16[1,2,512,128]{3,2,1,0:T(8,128)(2,1)S(1)}, bf16[1,2,512,128]{3,2,1,0:T(8,128)(2,1)}, u32[]{:S(2)}, u32[]{:S(2)}) collective-permute-start(bf16[1,2,512,128]{3,2,1,0:T(8,128)(2,1)S(1)} %pack.3.refs_0_), channel_id=1, source_target_pairs={{0,4},{1,5},{2,6},{3,7},{4,8},{5,9},{6,10},{7,11},{8,12},{9,13},{1... | collective-permute-start | bytes 786440 | tf_op jit(solution)/shard_map/ppermute | solution.py:248
  5.7 29.8 %collective-permute-start.12 = (bf16[2,2,512,128]{3,2,1,0:T(8,128)(2,1)S(1)}, bf16[2,2,512,128]{3,2,1,0:T(8,128)(2,1)S(1)}, u32[]{:S(2)}, u32[]{:S(2)}) collective-permute-start(bf16[2,2,512,128]{3,2,1,0:T(8,128)(2,1)S(1)} %get-tuple-element.17.refs_0_), channel_id=1, source_target_pairs={{0,4},{1,5},{2,6},{3,7},{4,8},{5,9},{6,10},{7,11},{8,12},{9,13},{1... | collective-permute-start | bytes 1572872 | tf_op jit(solution)/shard_map/ppermute | solution.py:248
  7.0 39.8 %collective-permute-start.8 = (bf16[2,2,512,128]{3,2,1,0:T(8,128)(2,1)S(1)}, bf16[2,2,512,128]{3,2,1,0:T(8,128)(2,1)S(1)}, u32[]{:S(2)}, u32[]{:S(2)}) collective-permute-start(bf16[2,2,512,128]{3,2,1,0:T(8,128)(2,1)S(1)} %get-tuple-element.16.refs_0_), channel_id=1, source_target_pairs={{0,4},{1,5},{2,6},{3,7},{4,8},{5,9},{6,10},{7,11},{8,12},{9,13},{1... | collective-permute-start | bytes 1572872 | tf_op jit(solution)/shard_map/ppermute | solution.py:248
  8.3 43.0 %collective-permute-start = (bf16[1,2,512,128]{3,2,1,0:T(8,128)(2,1)S(1)}, bf16[1,2,512,128]{3,2,1,0:T(8,128)(2,1)S(1)}, u32[]{:S(2)}, u32[]{:S(2)}) collective-permute-start(bf16[1,2,512,128]{3,2,1,0:T(8,128)(2,1)S(1)} %get-tuple-element.15.refs_0_), channel_id=1, source_target_pairs={{0,4},{1,5},{2,6},{3,7},{4,8},{5,9},{6,10},{7,11},{8,12},{9,13},{1... | collective-permute-start | bytes 786440 | tf_op jit(solution)/shard_map/ppermute | solution.py:248
  25.4 25.9 %collective-permute-start.5 = (bf16[1,2,512,128]{3,2,1,0:T(8,128)(2,1)S(1)}, bf16[1,2,512,128]{3,2,1,0:T(8,128)(2,1)S(1)}, u32[]{:S(2)}, u32[]{:S(2)}) collective-permute-start(bf16[1,2,512,128]{3,2,1,0:T(8,128)(2,1)S(1)} %get-tuple-element.26), channel_id=1, source_target_pairs={{0,2},{1,3},{6,4},{7,5},{4,6},{5,7},{10,8},{11,9},{8,10},{9,11},{1... | collective-permute-start | bytes 786440 | tf_op jit(solution)/shard_map/ppermute | solution.py:252
  28.8 26.2 %collective-permute-start.6 = (bf16[1,2,512,128]{3,2,1,0:T(8,128)(2,1)S(1)}, bf16[1,2,512,128]{3,2,1,0:T(8,128)(2,1)S(1)}, u32[]{:S(2)}, u32[]{:S(2)}) collective-permute-start(bf16[1,2,512,128]{3,2,1,0:T(8,128)(2,1)S(1)} %get-tuple-element.25), channel_id=1, source_target_pairs={{1,0},{0,1},{3,2},{2,3},{5,4},{4,5},{7,6},{6,7},{9,8},{8,9},{11,10... | collective-permute-start | bytes 786440 | tf_op jit(solution)/shard_map/ppermute | solution.py:253
  35.5 19.2 %collective-permute-start.17 = (bf16[2,2,512,128]{3,2,1,0:T(8,128)(2,1)S(1)}, bf16[2,2,512,128]{3,2,1,0:T(8,128)(2,1)S(1)}, u32[]{:S(2)}, u32[]{:S(2)}) collective-permute-start(bf16[2,2,512,128]{3,2,1,0:T(8,128)(2,1)S(1)} %get-tuple-element.20), channel_id=1, source_target_pairs={{0,2},{1,3},{6,4},{7,5},{4,6},{5,7},{10,8},{11,9},{8,10},{9,11},{1... | collective-permute-start | bytes 1572872 | tf_op jit(solution)/shard_map/ppermute | solution.py:252
  46.8 16.7 %collective-permute-start.13 = (bf16[2,2,512,128]{3,2,1,0:T(8,128)(2,1)S(1)}, bf16[2,2,512,128]{3,2,1,0:T(8,128)(2,1)S(1)}, u32[]{:S(2)}, u32[]{:S(2)}) collective-permute-start(bf16[2,2,512,128]{3,2,1,0:T(8,128)(2,1)S(1)} %get-tuple-element.22), channel_id=1, source_target_pairs={{0,2},{1,3},{6,4},{7,5},{4,6},{5,7},{10,8},{11,9},{8,10},{9,11},{1... | collective-permute-start | bytes 1572872 | tf_op jit(solution)/shard_map/ppermute | solution.py:252
  51.2 16.8 %collective-permute-start.18 = (bf16[2,2,512,128]{3,2,1,0:T(8,128)(2,1)S(1)}, bf16[2,2,512,128]{3,2,1,0:T(8,128)(2,1)S(1)}, u32[]{:S(2)}, u32[]{:S(2)}) collective-permute-start(bf16[2,2,512,128]{3,2,1,0:T(8,128)(2,1)S(1)} %get-tuple-element.19), channel_id=1, source_target_pairs={{1,0},{0,1},{3,2},{2,3},{5,4},{4,5},{7,6},{6,7},{9,8},{8,9},{11,10... | collective-permute-start | bytes 1572872 | tf_op jit(solution)/shard_map/ppermute | solution.py:253
  51.3 20.4 %collective-permute-start.9 = (bf16[2,2,512,128]{3,2,1,0:T(8,128)(2,1)S(1)}, bf16[2,2,512,128]{3,2,1,0:T(8,128)(2,1)S(1)}, u32[]{:S(2)}, u32[]{:S(2)}) collective-permute-start(bf16[2,2,512,128]{3,2,1,0:T(8,128)(2,1)S(1)} %get-tuple-element.24), channel_id=1, source_target_pairs={{0,2},{1,3},{6,4},{7,5},{4,6},{5,7},{10,8},{11,9},{8,10},{9,11},{1... | collective-permute-start | bytes 1572872 | tf_op jit(solution)/shard_map/ppermute | solution.py:252
  54.7 17.3 %collective-permute-start.19 = (bf16[2,2,512,128]{3,2,1,0:T(8,128)(2,1)S(1)}, bf16[2,2,512,128]{3,2,1,0:T(8,128)(2,1)S(1)}, u32[]{:S(2)}, u32[]{:S(2)}) collective-permute-start(bf16[2,2,512,128]{3,2,1,0:T(8,128)(2,1)S(1)} %collective-permute-done.17.refs_1_), channel_id=1, source_target_pairs={{1,0},{0,1},{3,2},{2,3},{5,4},{4,5},{7,6},{6,7},{9,8},{8,9},{11,10... | collective-permute-start | bytes 1572872 | tf_op jit(solution)/shard_map/ppermute | solution.py:254
  55.0 3.7 %collective-permute-start.7 = (bf16[1,2,512,128]{3,2,1,0:T(8,128)(2,1)S(1)}, bf16[1,2,512,128]{3,2,1,0:T(8,128)(2,1)S(1)}, u32[]{:S(2)}, u32[]{:S(2)}) collective-permute-start(bf16[1,2,512,128]{3,2,1,0:T(8,128)(2,1)S(1)} %collective-permute-done.5.refs_1_), channel_id=1, source_target_pairs={{1,0},{0,1},{3,2},{2,3},{5,4},{4,5},{7,6},{6,7},{9,8},{8,9},{11,10... | collective-permute-start | bytes 786440 | tf_op jit(solution)/shard_map/ppermute | solution.py:254
  58.7 21.7 %collective-permute-start.14 = (bf16[2,2,512,128]{3,2,1,0:T(8,128)(2,1)S(1)}, bf16[2,2,512,128]{3,2,1,0:T(8,128)(2,1)S(1)}, u32[]{:S(2)}, u32[]{:S(2)}) collective-permute-start(bf16[2,2,512,128]{3,2,1,0:T(8,128)(2,1)S(1)} %get-tuple-element.21), channel_id=1, source_target_pairs={{1,0},{0,1},{3,2},{2,3},{5,4},{4,5},{7,6},{6,7},{9,8},{8,9},{11,10... | collective-permute-start | bytes 1572872 | tf_op jit(solution)/shard_map/ppermute | solution.py:253
  63.4 17.2 %collective-permute-start.15 = (bf16[2,2,512,128]{3,2,1,0:T(8,128)(2,1)S(1)}, bf16[2,2,512,128]{3,2,1,0:T(8,128)(2,1)S(1)}, u32[]{:S(2)}, u32[]{:S(2)}) collective-permute-start(bf16[2,2,512,128]{3,2,1,0:T(8,128)(2,1)S(1)} %collective-permute-done.13.refs_1_), channel_id=1, source_target_pairs={{1,0},{0,1},{3,2},{2,3},{5,4},{4,5},{7,6},{6,7},{9,8},{8,9},{11,10... | collective-permute-start | bytes 1572872 | tf_op jit(solution)/shard_map/ppermute | solution.py:254
  68.0 12.0 %collective-permute-start.1 = (bf16[1,2,512,128]{3,2,1,0:T(8,128)(2,1)S(1)}, bf16[1,2,512,128]{3,2,1,0:T(8,128)(2,1)S(1)}, u32[]{:S(2)}, u32[]{:S(2)}) collective-permute-start(bf16[1,2,512,128]{3,2,1,0:T(8,128)(2,1)S(1)} %get-tuple-element.28), channel_id=1, source_target_pairs={{0,2},{1,3},{6,4},{7,5},{4,6},{5,7},{10,8},{11,9},{8,10},{9,11},{1... | collective-permute-start | bytes 786440 | tf_op jit(solution)/shard_map/ppermute | solution.py:252
  71.7 15.8 %collective-permute-start.10 = (bf16[2,2,512,128]{3,2,1,0:T(8,128)(2,1)S(1)}, bf16[2,2,512,128]{3,2,1,0:T(8,128)(2,1)S(1)}, u32[]{:S(2)}, u32[]{:S(2)}) collective-permute-start(bf16[2,2,512,128]{3,2,1,0:T(8,128)(2,1)S(1)} %get-tuple-element.23), channel_id=1, source_target_pairs={{1,0},{0,1},{3,2},{2,3},{5,4},{4,5},{7,6},{6,7},{9,8},{8,9},{11,10... | collective-permute-start | bytes 1572872 | tf_op jit(solution)/shard_map/ppermute | solution.py:253
  71.9 15.5 %collective-permute-start.11 = (bf16[2,2,512,128]{3,2,1,0:T(8,128)(2,1)S(1)}, bf16[2,2,512,128]{3,2,1,0:T(8,128)(2,1)S(1)}, u32[]{:S(2)}, u32[]{:S(2)}) collective-permute-start(bf16[2,2,512,128]{3,2,1,0:T(8,128)(2,1)S(1)} %collective-permute-done.9.refs_1_), channel_id=1, source_target_pairs={{1,0},{0,1},{3,2},{2,3},{5,4},{4,5},{7,6},{6,7},{9,8},{8,9},{11,10... | collective-permute-start | bytes 1572872 | tf_op jit(solution)/shard_map/ppermute | solution.py:254
  80.1 14.2 %collective-permute-start.2 = (bf16[1,2,512,128]{3,2,1,0:T(8,128)(2,1)S(1)}, bf16[1,2,512,128]{3,2,1,0:T(8,128)(2,1)S(1)}, u32[]{:S(2)}, u32[]{:S(2)}) collective-permute-start(bf16[1,2,512,128]{3,2,1,0:T(8,128)(2,1)S(1)} %get-tuple-element.27), channel_id=1, source_target_pairs={{1,0},{0,1},{3,2},{2,3},{5,4},{4,5},{7,6},{6,7},{9,8},{8,9},{11,10... | collective-permute-start | bytes 786440 | tf_op jit(solution)/shard_map/ppermute | solution.py:253
  80.4 14.0 %collective-permute-start.3 = (bf16[1,2,512,128]{3,2,1,0:T(8,128)(2,1)S(1)}, bf16[1,2,512,128]{3,2,1,0:T(8,128)(2,1)S(1)}, u32[]{:S(2)}, u32[]{:S(2)}) collective-permute-start(bf16[1,2,512,128]{3,2,1,0:T(8,128)(2,1)S(1)} %collective-permute-done.1.refs_1_), channel_id=1, source_target_pairs={{1,0},{0,1},{3,2},{2,3},{5,4},{4,5},{7,6},{6,7},{9,8},{8,9},{11,10... | collective-permute-start | bytes 786440 | tf_op jit(solution)/shard_map/ppermute | solution.py:254
